TPU v7x, 512 devices: a whole 4x8x8 slice. The times are simulated.
512 devices in a mesh: row: 8 (over y), col: 16 (over x, z_hi, core), layer: 4 (over z_lo).
Axes of the slice: x: 4, y: 8, z: 8 (z_hi: 2, z_lo: 4; z = z_hi * 4 + z_lo), core: 2. Of those that a mesh axis runs over, the one named last changes fastest.
Arguments:
- sign_iterate: bfloat16 [8192, 8192], P('row', 'col'), may hold values from -0.109375 to 0.109375
- square: bfloat16 [8192, 8192], P('row', 'col'), may hold values from -6 to 6
- pattern: int32 [64, 64], replicated, may hold values 0 or 1
- keep: int32 [64, 64], replicated, may hold values from 0 to 1, as said below
Outputs:
- product: bfloat16 [8192, 8192], P(('row', 'layer'), 'col')
Inputs may be any that keep to these rules, and one draw needn't show every extreme that they name: In every region of 2 block rows by 4 block columns, aligned to the output's shards along row+layer and col, exactly 6 blocks have keep 1.
All inputs are finite; a program needn't handle non-finite values.
Results may differ from a plain program's by a relative error of at most 0.001.
Values may be sent and summed in bfloat16 or wider, within the bound.
No kernel may reach another device: no remote copies, remote signals or barrier semaphores. Data moves between devices by JAX's collectives and lax.ppermute only.
A program may use at most 64 MiB of HBM per device.

v0:
```python
import functools

import jax
import jax.numpy as jnp
from jax import lax
from jax.experimental import pallas as pl
from jax.experimental.pallas import tpu as pltpu
from jax.sharding import PartitionSpec as P


BLK = 128
AXES = ("row", "col", "layer")
ROWS, XS, LAYERS = 8, 4, 4
KEPT = 6
EXTRA = 16
LEVELS = 32000.0


def table(move):
    pairs = []
    for r in range(ROWS):
        for x in range(XS):
            for z in range(2):
                for k in range(2):
                    for l in range(LAYERS):
                        r2, x2, z2, k2, l2 = move(r, x, z, k, l)
                        here = (r * 16 + x * 4 + z * 2 + k) * LAYERS + l
                        there = ((r2 % ROWS) * 16 + (x2 % XS) * 4 + z2 * 2 + k2) * LAYERS + l2
                        pairs.append((here, there))
    return pairs


ALONG_Y = table(lambda r, x, z, k, l: (r + 1 - 2 * k, x, z, k, l))
ALONG_X = table(lambda r, x, z, k, l: (r, x + 1 - 2 * k, z, k, l))
ACROSS_Z = table(lambda r, x, z, k, l: (r, x, 1 - z, k, l ^ 2))
OTHER_CORE = table(lambda r, x, z, k, l: (r, x, z, 1 - k, l))
CORE_PAIRS = [[2 * i, 2 * i + 1] for i in range(8)]


def both_cores(value):
    return lax.all_gather(value, "col", axis=0, tiled=False, axis_index_groups=CORE_PAIRS)


def assemble_kernel(at_ref, s0_ref, s1_ref, s2_ref, s3_ref, s1o_ref, s2o_ref, s3o_ref, s4_ref, ss_ref, sems):
    y, k = at_ref[0], at_ref[3]
    d = 1 - 2 * k
    pieces = [
        (s0_ref, y), (s1_ref, y - d), (s2_ref, y - 2 * d), (s3_ref, y - 3 * d),
        (s1o_ref, y + d), (s2o_ref, y + 2 * d), (s3o_ref, y + 3 * d), (s4_ref, y + 4),
    ]
    copies = [
        pltpu.make_async_copy(piece.at[k], ss_ref.at[lax.rem(row + 16, 8)], sems.at[i])
        for i, (piece, row) in enumerate(pieces)
    ]
    for c in copies:
        c.start()
    for c in copies:
        c.wait()


def assemble(at, pieces):
    anywhere = pl.BlockSpec(memory_space=pl.ANY)
    return pl.pallas_call(
        assemble_kernel,
        out_shape=jax.ShapeDtypeStruct((ROWS, 2 * BLK, 4 * BLK), jnp.bfloat16),
        in_specs=[pl.BlockSpec(memory_space=pltpu.SMEM)] + [anywhere] * 8,
        out_specs=pl.BlockSpec(memory_space=pltpu.VMEM),
        scratch_shapes=[pltpu.SemaphoreType.DMA((8,))],
        compiler_params=pltpu.CompilerParams(vmem_limit_bytes=6 * 2**20),
        cost_estimate=pl.CostEstimate(flops=0, bytes_accessed=4 * 2**20, transcendentals=0),
        name="assemble",
    )(at, *pieces)


def region_kernel(shift, at_ref, mask_ref, keep_ref, x0_ref, x1_ref, x1o_ref, x2_ref, ss_ref, out_ref, xs_ref):
    x, z, k, l = (at_ref[i] for i in range(1, 5))
    d = 1 - 2 * k
    j = lax.rem(l + shift, LAYERS)
    for slab, x_at in ((x0_ref, x), (x1_ref, x - d), (x1o_ref, x + d), (x2_ref, x + 2)):
        for zsel in range(2):
            row = 2 * lax.rem(x_at + 8, 4) + lax.rem(z + zsel, 2)
            for g in range(2):
                which = row * 2 + g
                column = pl.ds(pl.multiple_of(which * BLK, BLK), BLK)
                for a in range(2):
                    part = slab[zsel, g, a * BLK:(a + 1) * BLK, :]
                    stored = jnp.where(mask_ref[j * 2 + a, which] == 1, part, jnp.zeros_like(part))
                    xs_ref[a * BLK:(a + 1) * BLK, column] = stored
    value = jnp.dot(xs_ref[...], ss_ref[...].reshape(2048, 512), preferred_element_type=jnp.float32)
    flags = [keep_ref[j * 2 + a, b] == 1 for a in range(2) for b in range(4)]
    blocks = [value[a * BLK:(a + 1) * BLK, b * BLK:(b + 1) * BLK] for a in range(2) for b in range(4)]
    if shift:
        top = jnp.zeros((8, BLK), jnp.float32)
        for flag, block in zip(flags, blocks):
            high = jnp.max(jnp.abs(block).reshape(BLK // 8, 8, BLK), axis=0)
            top = jnp.maximum(top, jnp.where(flag, high, 0.0))
        top = jnp.max(top, axis=(0, 1), keepdims=True)
        level = jnp.ceil(8.0 * jnp.log2(jnp.maximum(top, 1e-30)))
        level = jnp.broadcast_to(level, (EXTRA, BLK))
        factor = (jnp.exp2(level * -0.125) * LEVELS)[0:1, :]
        out_ref[pl.ds(KEPT * BLK, EXTRA), :] = level.astype(jnp.int32).astype(jnp.int16)
        blocks = [jnp.round(block * factor).astype(jnp.int32).astype(jnp.int16) for block in blocks]
    at = jnp.int32(0)
    for flag, block in zip(flags, blocks):
        spot = pl.ds(pl.multiple_of(at * BLK, BLK), BLK)

        @pl.when(flag)
        def _():
            out_ref[spot, :] = block

        at = at + flag.astype(jnp.int32)


def region(shift, at, mask, keep, xs, ss):
    rows = pl.BlockSpec(
        (2, 2, 2 * BLK, BLK), lambda i, at, mask, keep: (0, 0, lax.rem(at[4] + shift, LAYERS), 0)
    )
    whole = pl.BlockSpec(memory_space=pltpu.VMEM)
    shape = (KEPT * BLK + EXTRA, BLK) if shift else (KEPT * BLK, BLK)
    return pl.pallas_call(
        functools.partial(region_kernel, shift),
        out_shape=jax.ShapeDtypeStruct(shape, jnp.int16 if shift else jnp.float32),
        grid_spec=pltpu.PrefetchScalarGridSpec(
            num_scalar_prefetch=3,
            grid=(1,),
            in_specs=[rows] * 4 + [whole],
            out_specs=whole,
            scratch_shapes=[pltpu.VMEM((2 * BLK, 2048), jnp.bfloat16)],
        ),
        compiler_params=pltpu.CompilerParams(vmem_limit_bytes=12 * 2**20),
        cost_estimate=pl.CostEstimate(flops=2 * 256 * 2048 * 512, bytes_accessed=4 * 2**20, transcendentals=0),
    )(at, mask, keep, *xs, ss)


def finish_kernel(at_ref, keep_ref, own_ref, *refs):
    *got_refs, out_ref = refs
    l = at_ref[4]
    scales = []
    for got in got_refs:
        level = got[pl.ds(KEPT * BLK, EXTRA), :].astype(jnp.int32).astype(jnp.float32)
        scales.append((jnp.exp2(level * 0.125) * (1.0 / LEVELS))[0:1, :])
    at = jnp.int32(0)
    for a in range(2):
        for b in range(4):
            flag = keep_ref[l * 2 + a, b] == 1
            spot = pl.ds(pl.multiple_of(jnp.minimum(at, KEPT - 1) * BLK, BLK), BLK)
            total = own_ref[spot, :]
            for got, scale in zip(got_refs, scales):
                total = total + got[spot, :].astype(jnp.int32).astype(jnp.float32) * scale
            total = jnp.where(flag, total, 0.0)
            out_ref[a * BLK:(a + 1) * BLK, b * BLK:(b + 1) * BLK] = total.astype(jnp.bfloat16)
            at = at + flag.astype(jnp.int32)


def finish(at, keep, own, got):
    smem = pl.BlockSpec(memory_space=pltpu.SMEM)
    vmem = pl.BlockSpec(memory_space=pltpu.VMEM)
    return pl.pallas_call(
        finish_kernel,
        out_shape=jax.ShapeDtypeStruct((2 * BLK, 4 * BLK), jnp.bfloat16),
        in_specs=[smem, smem] + [vmem] * 4,
        out_specs=vmem,
        compiler_params=pltpu.CompilerParams(vmem_limit_bytes=8 * 2**20),
        cost_estimate=pl.CostEstimate(flops=2**20, bytes_accessed=2 * 2**20, transcendentals=0),
        name="finish",
    )(at, keep, own, *got)


def body(sign_iterate, square, pattern, keep):
    l = lax.axis_index("layer")
    y = lax.axis_index("row")
    c = lax.axis_index("col")
    k = c % 2
    at = jnp.stack([y, c // 4, (c // 2) % 2, k, l]).astype(jnp.int32)
    mask = lax.dynamic_slice(pattern, (y * 8, 0), (8, 64)).reshape(8, 16, 4)
    mask = lax.dynamic_index_in_dim(mask, l, 2, False)
    keep_here = lax.dynamic_slice(keep, (y * 8, c * 4), (8, 4))

    def step(value, pairs):
        return lax.ppermute(value, AXES, pairs)

    x_other = lax.dynamic_slice_in_dim(sign_iterate, (l ^ 2) * BLK, BLK, 1)
    x_z = step(x_other, ACROSS_Z)
    s_own = lax.dynamic_index_in_dim(square.reshape(2, LAYERS, BLK, 512), l, 1, False).reshape(256, 512)
    s0 = both_cores(s_own)
    s1 = step(s0, ALONG_Y)
    x_own = lax.dynamic_slice_in_dim(sign_iterate, l * BLK, BLK, 1)
    x0 = jnp.stack([both_cores(x_own), both_cores(x_z)])
    x1 = step(x0, ALONG_X)
    s2 = step(s1, ALONG_Y)
    s1o = step(s1, OTHER_CORE)
    s3 = step(s2, ALONG_Y)
    s2o = step(s2, OTHER_CORE)
    x2 = step(x1, ALONG_X)
    s4 = step(s3, ALONG_Y)
    x1o = step(x1, OTHER_CORE)
    s3o = step(s3, OTHER_CORE)
    ss = assemble(at, (s0, s1, s2, s3, s1o, s2o, s3o, s4))
    xs = (x0, x1, x1o, x2)
    got = []
    for shift in (2, 1, 3):
        part = region(shift, at, mask, keep_here, xs, ss)
        pairs = table(lambda r, x, z, k, l, shift=shift: (r, x, z, k, (l + shift) % LAYERS))
        got.append(step(part, pairs))
    own = region(0, at, mask, keep_here, xs, ss)
    return finish(at, keep_here, own, got)


def solution(mesh):
    return jax.shard_map(
        body,
        mesh=mesh,
        in_specs=(P("row", "col"), P("row", "col"), P(), P()),
        out_specs=P(("row", "layer"), "col"),
        check_vma=False,
    )
```

profile of v0, /device:TPU:1, one launch (start us, length us, event | category | flops | bytes accessed | tf_op | source)
XLA Modules:
  0.0 103.1 jit_solution(9749005816157034619)
XLA Ops:
  0.0 0.0 copy-start
  0.0 1.2 %constant_dynamic-slice_fusion.2 = (bf16[1024,128]{1,0:T(8,128)(2,1)S(1)}, bf16[1024,128]{1,0:T(8,128)(2,1)S(1)}) fusion(bf16[1024,512]{1,0:T(8,128)(2,1)} %param.4, s32[]{:T(128)S(6)} %select_n.44, s32[]{:T(128)S(6)} %select_n.45), kind=kLoop, calls=%fused_computation.3 | loop fusion | bytes 1048584 | tf_op jit(solution)/shard_map/dynamic_slice | solution.py:187
  1.2 11.5 %collective-permute-start = (bf16[1024,128]{1,0:T(8,128)(2,1)S(1)}, bf16[1024,128]{1,0:T(8,128)(2,1)S(1)}, u32[]{:S(2)}, u32[]{:S(2)}) collective-permute-start(bf16[1024,128]{1,0:T(8,128)(2,1)S(1)} %get-tuple-element.6), channel_id=1, source_target_pairs={{0,10},{1,11},{2,8},{3,9},{4,14},{5,15},{6,12},{7,13},{8,2},{9,3},... | collective-permute-start | bytes 786440 | tf_op jit(solution)/shard_map/ppermute | solution.py:180
  12.7 0.0 copy-done
  12.7 2.8 %all_gather.19.s0_ref = bf16[2,256,512]{2,1,0:T(8,128)(2,1)S(1)} all-gather(bf16[1,256,512]{2,1,0:T(8,128)(2,1)S(1)} %bitcast.20), channel_id=1, replica_groups={{0,4},{8,12},{16,20},{24,28},{32,36},{40,44},{48,52},{56,60},{1,5},{9,1..., dimensions={0}, use_global_device_ids=true | all-gather | bytes 786432 | tf_op jit(solution)/shard_map/all_gather | solution.py:41
  15.5 0.0 copy-start.1
  15.5 5.1 %collective-permute-start.4 = (bf16[2,256,512]{2,1,0:T(8,128)(2,1)S(1)}, bf16[2,256,512]{2,1,0:T(8,128)(2,1)S(1)}, u32[]{:S(2)}, u32[]{:S(2)}) collective-permute-start(bf16[2,256,512]{2,1,0:T(8,128)(2,1)S(1)} %all_gather.19.s0_ref), channel_id=1, source_target_pairs={{0,64},{1,65},{2,66},{3,67},{4,452},{5,453},{6,454},{7,455},{8,72}... | collective-permute-start | bytes 1572872 | tf_op jit(solution)/shard_map/ppermute | solution.py:180
  20.6 2.2 %all-gather = bf16[2048,128]{1,0:T(8,128)(2,1)S(1)} all-gather(bf16[1024,128]{1,0:T(8,128)(2,1)S(1)} %get-tuple-element.5), channel_id=2, replica_groups={{0,4},{8,12},{16,20},{24,28},{32,36},{40,44},{48,52},{56,60},{1,5},{9,1..., dimensions={0}, use_global_device_ids=true | all-gather | bytes 786432 | tf_op jit(solution)/shard_map/all_gather | solution.py:41
  22.7 0.6 collective-permute-done
  23.4 3.2 %all-gather.1 = bf16[2048,128]{1,0:T(8,128)(2,1)S(1)} all-gather(bf16[1024,128]{1,0:T(8,128)(2,1)S(1)} %collective-permute-done), channel_id=3, replica_groups={{0,4},{8,12},{16,20},{24,28},{32,36},{40,44},{48,52},{56,60},{1,5},{9,1..., dimensions={0}, use_global_device_ids=true | all-gather | bytes 786432 | tf_op jit(solution)/shard_map/all_gather | solution.py:41
  26.6 0.1 pad_maximum_fusion.x0_ref
  26.7 4.4 %collective-permute-start.1 = (bf16[2,2,1024,128]{3,2,1,0:T(8,128)(2,1)S(1)}, bf16[2,2,1024,128]{3,2,1,0:T(8,128)(2,1)S(1)}, u32[]{:S(2)}, u32[]{:S(2)}) collective-permute-start(bf16[2,2,1024,128]{3,2,1,0:T(8,128)(2,1)S(1)} %pad_maximum_fusion.x0_ref), channel_id=1, source_target_pairs={{0,16},{1,17},{2,18},{3,19},{4,52},{5,53},{6,54},{7,55},{8,24},{9,... | collective-permute-start | bytes 3145736 | tf_op jit(solution)/shard_map/ppermute | solution.py:180
  31.1 0.0 collective-permute-done.4.s1_ref
  31.1 5.1 %collective-permute-start.5 = (bf16[2,256,512]{2,1,0:T(8,128)(2,1)S(1)}, bf16[2,256,512]{2,1,0:T(8,128)(2,1)}, u32[]{:S(2)}, u32[]{:S(2)}) collective-permute-start(bf16[2,256,512]{2,1,0:T(8,128)(2,1)S(1)} %collective-permute-done.4.s1_ref), channel_id=1, source_target_pairs={{0,64},{1,65},{2,66},{3,67},{4,452},{5,453},{6,454},{7,455},{8,72}... | collective-permute-start | bytes 1572872 | tf_op jit(solution)/shard_map/ppermute | solution.py:180
  36.2 6.1 %collective-permute-done.5.s2_ref = bf16[2,256,512]{2,1,0:T(8,128)(2,1)} collective-permute-done((bf16[2,256,512]{2,1,0:T(8,128)(2,1)S(1)}, bf16[2,256,512]{2,1,0:T(8,128)(2,1)}, u32[]{:S(2)}, u32[]{:S(2)}) %collective-permute-start.5) | collective-permute-done | bytes 524320 | tf_op jit(solution)/shard_map/ppermute | solution.py:180
  42.3 5.3 %collective-permute-start.6 = (bf16[2,256,512]{2,1,0:T(8,128)(2,1)}, bf16[2,256,512]{2,1,0:T(8,128)(2,1)}, u32[]{:S(2)}, u32[]{:S(2)}) collective-permute-start(bf16[2,256,512]{2,1,0:T(8,128)(2,1)} %collective-permute-done.5.s2_ref), channel_id=1, source_target_pairs={{0,64},{1,65},{2,66},{3,67},{4,452},{5,453},{6,454},{7,455},{8,72}... | collective-permute-start | bytes 1572872 | tf_op jit(solution)/shard_map/ppermute | solution.py:180
  47.6 1.9 %collective-permute-start.7 = (bf16[2,256,512]{2,1,0:T(8,128)(2,1)S(1)}, bf16[2,256,512]{2,1,0:T(8,128)(2,1)S(1)}, u32[]{:S(2)}, u32[]{:S(2)}) collective-permute-start(bf16[2,256,512]{2,1,0:T(8,128)(2,1)S(1)} %collective-permute-done.4.s1_ref), channel_id=1, source_target_pairs={{0,4},{1,5},{2,6},{3,7},{4,0},{5,1},{6,2},{7,3},{8,12},{9,13},{10,... | collective-permute-start | bytes 1572872 | tf_op jit(solution)/shard_map/ppermute | solution.py:180
  49.5 0.0 copy-start.3
  49.5 0.8 copy-done.3
  50.3 0.0 collective-permute-done.1.x1_ref
  50.3 0.0 copy-done.1
  50.3 2.4 %collective-permute-start.2 = (bf16[2,2,1024,128]{3,2,1,0:T(8,128)(2,1)S(1)}, bf16[2,2,1024,128]{3,2,1,0:T(8,128)(2,1)}, u32[]{:S(2)}, u32[]{:S(2)}) collective-permute-start(bf16[2,2,1024,128]{3,2,1,0:T(8,128)(2,1)S(1)} %collective-permute-done.1.x1_ref), channel_id=1, source_target_pairs={{0,4},{1,5},{2,6},{3,7},{4,0},{5,1},{6,2},{7,3},{8,12},{9,13},{10,... | collective-permute-start | bytes 3145736 | tf_op jit(solution)/shard_map/ppermute | solution.py:180
  52.7 2.3 %collective-permute-start.3 = (bf16[2,2,1024,128]{3,2,1,0:T(8,128)(2,1)S(1)}, bf16[2,2,1024,128]{3,2,1,0:T(8,128)(2,1)}, u32[]{:S(2)}, u32[]{:S(2)}) collective-permute-start(bf16[2,2,1024,128]{3,2,1,0:T(8,128)(2,1)S(1)} %collective-permute-done.1.x1_ref), channel_id=1, source_target_pairs={{0,16},{1,17},{2,18},{3,19},{4,52},{5,53},{6,54},{7,55},{8,24},{9,... | collective-permute-start | bytes 3145736 | tf_op jit(solution)/shard_map/ppermute | solution.py:180
  55.0 1.9 %collective-permute-start.8 = (bf16[2,256,512]{2,1,0:T(8,128)(2,1)}, bf16[2,256,512]{2,1,0:T(8,128)(2,1)}, u32[]{:S(2)}, u32[]{:S(2)}) collective-permute-start(bf16[2,256,512]{2,1,0:T(8,128)(2,1)} %collective-permute-done.5.s2_ref), channel_id=1, source_target_pairs={{0,4},{1,5},{2,6},{3,7},{4,0},{5,1},{6,2},{7,3},{8,12},{9,13},{10,... | collective-permute-start | bytes 1572872 | tf_op jit(solution)/shard_map/ppermute | solution.py:180
  56.9 0.0 collective-permute-done.6.s3_ref
  56.9 3.4 %collective-permute-start.10 = (bf16[2,256,512]{2,1,0:T(8,128)(2,1)}, bf16[2,256,512]{2,1,0:T(8,128)(2,1)}, u32[]{:S(2)}, u32[]{:S(2)}) collective-permute-start(bf16[2,256,512]{2,1,0:T(8,128)(2,1)} %collective-permute-done.6.s3_ref), channel_id=1, source_target_pairs={{0,64},{1,65},{2,66},{3,67},{4,452},{5,453},{6,454},{7,455},{8,72}... | collective-permute-start | bytes 1572872 | tf_op jit(solution)/shard_map/ppermute | solution.py:180
  60.3 0.0 collective-permute-done.7.s1o_ref
  60.3 0.0 copy-start.5
  60.4 0.8 copy-done.5
  61.2 1.9 %collective-permute-start.9 = (bf16[2,256,512]{2,1,0:T(8,128)(2,1)}, bf16[2,256,512]{2,1,0:T(8,128)(2,1)}, u32[]{:S(2)}, u32[]{:S(2)}) collective-permute-start(bf16[2,256,512]{2,1,0:T(8,128)(2,1)} %collective-permute-done.6.s3_ref), channel_id=1, source_target_pairs={{0,4},{1,5},{2,6},{3,7},{4,0},{5,1},{6,2},{7,3},{8,12},{9,13},{10,... | collective-permute-start | bytes 1572872 | tf_op jit(solution)/shard_map/ppermute | solution.py:180
  63.1 0.7 constant_dynamic-slice_fusion.4
  63.8 0.1 copy.9
  63.9 0.1 copy.10
  64.0 0.8 dynamic_slice.20.keep_ref
  64.7 0.1 stack.32.at_ref
  64.8 0.0 collective-permute-done.8.s2o_ref
  64.8 2.6 %collective-permute-done.10.s4_ref = bf16[2,256,512]{2,1,0:T(8,128)(2,1)} collective-permute-done((bf16[2,256,512]{2,1,0:T(8,128)(2,1)}, bf16[2,256,512]{2,1,0:T(8,128)(2,1)}, u32[]{:S(2)}, u32[]{:S(2)}) %collective-permute-start.10) | collective-permute-done | bytes 524320 | tf_op jit(solution)/shard_map/ppermute | solution.py:180
  67.5 0.0 collective-permute-done.9.s3o_ref
  67.5 0.0 copy-start.2
  67.5 1.0 %copy-done.2 = bf16[2,256,512]{2,1,0:T(8,128)(2,1)S(1)} copy-done((bf16[2,256,512]{2,1,0:T(8,128)(2,1)S(1)}, bf16[2,256,512]{2,1,0:T(8,128)(2,1)}, u32[]{:S(2)}) %copy-start.2) | copy-done | bytes 524312
  68.5 0.0 copy-start.4
  68.5 1.0 %copy-done.4 = bf16[2,256,512]{2,1,0:T(8,128)(2,1)S(1)} copy-done((bf16[2,256,512]{2,1,0:T(8,128)(2,1)S(1)}, bf16[2,256,512]{2,1,0:T(8,128)(2,1)}, u32[]{:S(2)}) %copy-start.4) | copy-done | bytes 524312
  69.6 0.0 copy-start.6
  69.6 1.0 %copy-done.6 = bf16[2,256,512]{2,1,0:T(8,128)(2,1)S(1)} copy-done((bf16[2,256,512]{2,1,0:T(8,128)(2,1)S(1)}, bf16[2,256,512]{2,1,0:T(8,128)(2,1)}, u32[]{:S(2)}) %copy-start.6) | copy-done | bytes 524312
  70.6 1.9 %assemble.1.ss_ref = bf16[8,256,512]{2,1,0:T(8,128)(2,1)S(1)} custom-call(s32[5]{0:T(128)S(1)} %stack.32.at_ref, bf16[2,256,512]{2,1,0:T(8,128)(2,1)S(1)} %copy-done.2, bf16[2,256,512]{2,1,0:T(8,128)(2,1)S(1)} %copy-done.4, bf16[2,256,512]{2,1,0:T(8,128)(2,1)} %collective-permute-done.5.s2_ref, bf16[2,256,512]{2,1,0:T(8,128)(2,1)} %collective-permute-done.6.s3_ref, ...), custom_call_target="tpu_custom_call" | custom-call | bytes 4194304 | tf_op jit(solution)/shard_map/assemble/pallas_call | solution.py:63
  72.6 0.0 collective-permute-done.2.x1o_ref
  72.6 0.0 collective-permute-done.3.x2_ref
  72.6 3.0 %shard_map.49 = s16[784,128]{1,0:T(8,128)(2,1)S(1)} custom-call(s32[5]{0:T(128)S(1)} %stack.32.at_ref, s32[8,16]{1,0:T(8,128)S(1)} %bitcast.14, s32[8,4]{1,0:T(8,128)S(1)} %dynamic_slice.20.keep_ref, bf16[2,2,1024,128]{3,2,1,0:T(8,128)(2,1)S(1)} %pad_maximum_fusion.x0_ref, bf16[2,2,1024,128]{3,2,1,0:T(8,128)(2,1)S(1)} %collective-permute-done.1.x1_ref, ...), custom_call_target="tpu_custom_call" | custom-call | flops 536870912 | bytes 4194304 | tf_op jit(solution)/shard_map/pallas_call | solution.py:120
  75.6 3.1 %collective-permute-start.13 = (s16[784,128]{1,0:T(8,128)(2,1)S(1)}, s16[784,128]{1,0:T(8,128)(2,1)S(1)}, u32[]{:S(2)}, u32[]{:S(2)}) collective-permute-start(s16[784,128]{1,0:T(8,128)(2,1)S(1)} %shard_map.49), channel_id=1, source_target_pairs={{0,3},{1,0},{2,1},{3,2},{4,7},{5,4},{6,5},{7,6},{8,11},{9,8},{10,9... | collective-permute-start | bytes 602120 | tf_op jit(solution)/shard_map/ppermute | solution.py:180
  78.7 3.0 %shard_map.48 = s16[784,128]{1,0:T(8,128)(2,1)S(1)} custom-call(s32[5]{0:T(128)S(1)} %stack.32.at_ref, s32[8,16]{1,0:T(8,128)S(1)} %bitcast.15, s32[8,4]{1,0:T(8,128)S(1)} %dynamic_slice.20.keep_ref, bf16[2,2,1024,128]{3,2,1,0:T(8,128)(2,1)S(1)} %pad_maximum_fusion.x0_ref, bf16[2,2,1024,128]{3,2,1,0:T(8,128)(2,1)S(1)} %collective-permute-done.1.x1_ref, ...), custom_call_target="tpu_custom_call" | custom-call | flops 536870912 | bytes 4194304 | tf_op jit(solution)/shard_map/pallas_call | solution.py:120
  81.7 2.7 %collective-permute-start.12 = (s16[784,128]{1,0:T(8,128)(2,1)S(1)}, s16[784,128]{1,0:T(8,128)(2,1)S(1)}, u32[]{:S(2)}, u32[]{:S(2)}) collective-permute-start(s16[784,128]{1,0:T(8,128)(2,1)S(1)} %shard_map.48), channel_id=1, source_target_pairs={{0,1},{1,2},{2,3},{3,0},{4,5},{5,6},{6,7},{7,4},{8,9},{9,10},{10,1... | collective-permute-start | bytes 602120 | tf_op jit(solution)/shard_map/ppermute | solution.py:180
  84.4 3.0 %shard_map.47 = s16[784,128]{1,0:T(8,128)(2,1)S(1)} custom-call(s32[5]{0:T(128)S(1)} %stack.32.at_ref, s32[8,16]{1,0:T(8,128)S(1)} %bitcast.16, s32[8,4]{1,0:T(8,128)S(1)} %dynamic_slice.20.keep_ref, bf16[2,2,1024,128]{3,2,1,0:T(8,128)(2,1)S(1)} %pad_maximum_fusion.x0_ref, bf16[2,2,1024,128]{3,2,1,0:T(8,128)(2,1)S(1)} %collective-permute-done.1.x1_ref, ...), custom_call_target="tpu_custom_call" | custom-call | flops 536870912 | bytes 4194304 | tf_op jit(solution)/shard_map/pallas_call | solution.py:120
  87.5 3.1 %collective-permute-start.11 = (s16[784,128]{1,0:T(8,128)(2,1)S(1)}, s16[784,128]{1,0:T(8,128)(2,1)S(1)}, u32[]{:S(2)}, u32[]{:S(2)}) collective-permute-start(s16[784,128]{1,0:T(8,128)(2,1)S(1)} %shard_map.47), channel_id=1, source_target_pairs={{0,2},{1,3},{2,0},{3,1},{4,6},{5,7},{6,4},{7,5},{8,10},{9,11},{10,... | collective-permute-start | bytes 602120 | tf_op jit(solution)/shard_map/ppermute | solution.py:180
  90.6 2.8 %shard_map.46.own_ref = f32[768,128]{1,0:T(8,128)S(1)} custom-call(s32[5]{0:T(128)S(1)} %stack.32.at_ref, s32[8,16]{1,0:T(8,128)S(1)} %bitcast.17, s32[8,4]{1,0:T(8,128)S(1)} %dynamic_slice.20.keep_ref, bf16[2,2,1024,128]{3,2,1,0:T(8,128)(2,1)S(1)} %pad_maximum_fusion.x0_ref, bf16[2,2,1024,128]{3,2,1,0:T(8,128)(2,1)S(1)} %collective-permute-done.1.x1_ref, ...), custom_call_target="tpu_custom_call" | custom-call | flops 536870912 | bytes 4194304 | tf_op jit(solution)/shard_map/pallas_call | solution.py:120
  93.4 0.0 collective-permute-done.13.refs_2_
  93.4 0.0 collective-permute-done.12.refs_1_
  93.4 8.1 %collective-permute-done.11.refs_0_ = s16[784,128]{1,0:T(8,128)(2,1)S(1)} collective-permute-done((s16[784,128]{1,0:T(8,128)(2,1)S(1)}, s16[784,128]{1,0:T(8,128)(2,1)S(1)}, u32[]{:S(2)}, u32[]{:S(2)}) %collective-permute-start.11) | collective-permute-done | bytes 200736 | tf_op jit(solution)/shard_map/ppermute | solution.py:180
  101.6 1.6 %finish.1 = bf16[256,512]{1,0:T(8,128)(2,1)} custom-call(s32[5]{0:T(128)S(1)} %stack.32.at_ref, s32[8,4]{1,0:T(8,128)S(1)} %dynamic_slice.20.keep_ref, f32[768,128]{1,0:T(8,128)S(1)} %shard_map.46.own_ref, s16[784,128]{1,0:T(8,128)(2,1)S(1)} %collective-permute-done.11.refs_0_, s16[784,128]{1,0:T(8,128)(2,1)S(1)} %collective-permute-done.12.refs_1_, ...), custom_call_target="tpu_custom_call" | custom-call | flops 1048576 | bytes 2097152 | tf_op jit(solution)/shard_map/finish/pallas_call | solution.py:158
  (2 shorter events, 0.0 us)
Async XLA Ops:
  0.0 12.7 %copy-start = (bf16[1024,512]{1,0:T(8,128)(2,1)S(1)}, bf16[1024,512]{1,0:T(8,128)(2,1)}, u32[]{:S(2)}) copy-start(bf16[1024,512]{1,0:T(8,128)(2,1)} %param.5) | copy-start | bytes 3145732
  1.2 22.2 %collective-permute-start = (bf16[1024,128]{1,0:T(8,128)(2,1)S(1)}, bf16[1024,128]{1,0:T(8,128)(2,1)S(1)}, u32[]{:S(2)}, u32[]{:S(2)}) collective-permute-start(bf16[1024,128]{1,0:T(8,128)(2,1)S(1)} %get-tuple-element.6), channel_id=1, source_target_pairs={{0,10},{1,11},{2,8},{3,9},{4,14},{5,15},{6,12},{7,13},{8,2},{9,3},... | collective-permute-start | bytes 786440 | tf_op jit(solution)/shard_map/ppermute | solution.py:180
  15.5 34.9 %copy-start.1 = (bf16[2,256,512]{2,1,0:T(8,128)(2,1)}, bf16[2,256,512]{2,1,0:T(8,128)(2,1)S(1)}, u32[]{:S(2)}) copy-start(bf16[2,256,512]{2,1,0:T(8,128)(2,1)S(1)} %all_gather.19.s0_ref) | copy-start | bytes 1572868
  15.5 15.6 %collective-permute-start.4 = (bf16[2,256,512]{2,1,0:T(8,128)(2,1)S(1)}, bf16[2,256,512]{2,1,0:T(8,128)(2,1)S(1)}, u32[]{:S(2)}, u32[]{:S(2)}) collective-permute-start(bf16[2,256,512]{2,1,0:T(8,128)(2,1)S(1)} %all_gather.19.s0_ref), channel_id=1, source_target_pairs={{0,64},{1,65},{2,66},{3,67},{4,452},{5,453},{6,454},{7,455},{8,72}... | collective-permute-start | bytes 1572872 | tf_op jit(solution)/shard_map/ppermute | solution.py:180
  26.7 23.6 %collective-permute-start.1 = (bf16[2,2,1024,128]{3,2,1,0:T(8,128)(2,1)S(1)}, bf16[2,2,1024,128]{3,2,1,0:T(8,128)(2,1)S(1)}, u32[]{:S(2)}, u32[]{:S(2)}) collective-permute-start(bf16[2,2,1024,128]{3,2,1,0:T(8,128)(2,1)S(1)} %pad_maximum_fusion.x0_ref), channel_id=1, source_target_pairs={{0,16},{1,17},{2,18},{3,19},{4,52},{5,53},{6,54},{7,55},{8,24},{9,... | collective-permute-start | bytes 3145736 | tf_op jit(solution)/shard_map/ppermute | solution.py:180
  31.1 11.2 %collective-permute-start.5 = (bf16[2,256,512]{2,1,0:T(8,128)(2,1)S(1)}, bf16[2,256,512]{2,1,0:T(8,128)(2,1)}, u32[]{:S(2)}, u32[]{:S(2)}) collective-permute-start(bf16[2,256,512]{2,1,0:T(8,128)(2,1)S(1)} %collective-permute-done.4.s1_ref), channel_id=1, source_target_pairs={{0,64},{1,65},{2,66},{3,67},{4,452},{5,453},{6,454},{7,455},{8,72}... | collective-permute-start | bytes 1572872 | tf_op jit(solution)/shard_map/ppermute | solution.py:180
  42.3 14.6 %collective-permute-start.6 = (bf16[2,256,512]{2,1,0:T(8,128)(2,1)}, bf16[2,256,512]{2,1,0:T(8,128)(2,1)}, u32[]{:S(2)}, u32[]{:S(2)}) collective-permute-start(bf16[2,256,512]{2,1,0:T(8,128)(2,1)} %collective-permute-done.5.s2_ref), channel_id=1, source_target_pairs={{0,64},{1,65},{2,66},{3,67},{4,452},{5,453},{6,454},{7,455},{8,72}... | collective-permute-start | bytes 1572872 | tf_op jit(solution)/shard_map/ppermute | solution.py:180
  47.6 12.7 %collective-permute-start.7 = (bf16[2,256,512]{2,1,0:T(8,128)(2,1)S(1)}, bf16[2,256,512]{2,1,0:T(8,128)(2,1)S(1)}, u32[]{:S(2)}, u32[]{:S(2)}) collective-permute-start(bf16[2,256,512]{2,1,0:T(8,128)(2,1)S(1)} %collective-permute-done.4.s1_ref), channel_id=1, source_target_pairs={{0,4},{1,5},{2,6},{3,7},{4,0},{5,1},{6,2},{7,3},{8,12},{9,13},{10,... | collective-permute-start | bytes 1572872 | tf_op jit(solution)/shard_map/ppermute | solution.py:180
  49.5 0.8 copy-start.3
  50.3 22.2 %collective-permute-start.2 = (bf16[2,2,1024,128]{3,2,1,0:T(8,128)(2,1)S(1)}, bf16[2,2,1024,128]{3,2,1,0:T(8,128)(2,1)}, u32[]{:S(2)}, u32[]{:S(2)}) collective-permute-start(bf16[2,2,1024,128]{3,2,1,0:T(8,128)(2,1)S(1)} %collective-permute-done.1.x1_ref), channel_id=1, source_target_pairs={{0,4},{1,5},{2,6},{3,7},{4,0},{5,1},{6,2},{7,3},{8,12},{9,13},{10,... | collective-permute-start | bytes 3145736 | tf_op jit(solution)/shard_map/ppermute | solution.py:180
  52.7 19.8 %collective-permute-start.3 = (bf16[2,2,1024,128]{3,2,1,0:T(8,128)(2,1)S(1)}, bf16[2,2,1024,128]{3,2,1,0:T(8,128)(2,1)}, u32[]{:S(2)}, u32[]{:S(2)}) collective-permute-start(bf16[2,2,1024,128]{3,2,1,0:T(8,128)(2,1)S(1)} %collective-permute-done.1.x1_ref), channel_id=1, source_target_pairs={{0,16},{1,17},{2,18},{3,19},{4,52},{5,53},{6,54},{7,55},{8,24},{9,... | collective-permute-start | bytes 3145736 | tf_op jit(solution)/shard_map/ppermute | solution.py:180
  55.0 9.8 %collective-permute-start.8 = (bf16[2,256,512]{2,1,0:T(8,128)(2,1)}, bf16[2,256,512]{2,1,0:T(8,128)(2,1)}, u32[]{:S(2)}, u32[]{:S(2)}) collective-permute-start(bf16[2,256,512]{2,1,0:T(8,128)(2,1)} %collective-permute-done.5.s2_ref), channel_id=1, source_target_pairs={{0,4},{1,5},{2,6},{3,7},{4,0},{5,1},{6,2},{7,3},{8,12},{9,13},{10,... | collective-permute-start | bytes 1572872 | tf_op jit(solution)/shard_map/ppermute | solution.py:180
  56.9 10.5 %collective-permute-start.10 = (bf16[2,256,512]{2,1,0:T(8,128)(2,1)}, bf16[2,256,512]{2,1,0:T(8,128)(2,1)}, u32[]{:S(2)}, u32[]{:S(2)}) collective-permute-start(bf16[2,256,512]{2,1,0:T(8,128)(2,1)} %collective-permute-done.6.s3_ref), channel_id=1, source_target_pairs={{0,64},{1,65},{2,66},{3,67},{4,452},{5,453},{6,454},{7,455},{8,72}... | collective-permute-start | bytes 1572872 | tf_op jit(solution)/shard_map/ppermute | solution.py:180
  60.3 0.8 copy-start.5
  61.2 6.3 %collective-permute-start.9 = (bf16[2,256,512]{2,1,0:T(8,128)(2,1)}, bf16[2,256,512]{2,1,0:T(8,128)(2,1)}, u32[]{:S(2)}, u32[]{:S(2)}) collective-permute-start(bf16[2,256,512]{2,1,0:T(8,128)(2,1)} %collective-permute-done.6.s3_ref), channel_id=1, source_target_pairs={{0,4},{1,5},{2,6},{3,7},{4,0},{5,1},{6,2},{7,3},{8,12},{9,13},{10,... | collective-permute-start | bytes 1572872 | tf_op jit(solution)/shard_map/ppermute | solution.py:180
  67.5 1.0 %copy-start.2 = (bf16[2,256,512]{2,1,0:T(8,128)(2,1)S(1)}, bf16[2,256,512]{2,1,0:T(8,128)(2,1)}, u32[]{:S(2)}) copy-start(bf16[2,256,512]{2,1,0:T(8,128)(2,1)} %copy-done.1) | copy-start | bytes 1572868
  68.5 1.0 %copy-start.4 = (bf16[2,256,512]{2,1,0:T(8,128)(2,1)S(1)}, bf16[2,256,512]{2,1,0:T(8,128)(2,1)}, u32[]{:S(2)}) copy-start(bf16[2,256,512]{2,1,0:T(8,128)(2,1)} %copy-done.3) | copy-start | bytes 1572868
  69.6 1.0 %copy-start.6 = (bf16[2,256,512]{2,1,0:T(8,128)(2,1)S(1)}, bf16[2,256,512]{2,1,0:T(8,128)(2,1)}, u32[]{:S(2)}) copy-start(bf16[2,256,512]{2,1,0:T(8,128)(2,1)} %copy-done.5) | copy-start | bytes 1572868
  75.6 17.8 %collective-permute-start.13 = (s16[784,128]{1,0:T(8,128)(2,1)S(1)}, s16[784,128]{1,0:T(8,128)(2,1)S(1)}, u32[]{:S(2)}, u32[]{:S(2)}) collective-permute-start(s16[784,128]{1,0:T(8,128)(2,1)S(1)} %shard_map.49), channel_id=1, source_target_pairs={{0,3},{1,0},{2,1},{3,2},{4,7},{5,4},{6,5},{7,6},{8,11},{9,8},{10,9... | collective-permute-start | bytes 602120 | tf_op jit(solution)/shard_map/ppermute | solution.py:180
  81.7 11.7 %collective-permute-start.12 = (s16[784,128]{1,0:T(8,128)(2,1)S(1)}, s16[784,128]{1,0:T(8,128)(2,1)S(1)}, u32[]{:S(2)}, u32[]{:S(2)}) collective-permute-start(s16[784,128]{1,0:T(8,128)(2,1)S(1)} %shard_map.48), channel_id=1, source_target_pairs={{0,1},{1,2},{2,3},{3,0},{4,5},{5,6},{6,7},{7,4},{8,9},{9,10},{10,1... | collective-permute-start | bytes 602120 | tf_op jit(solution)/shard_map/ppermute | solution.py:180
  87.5 14.1 %collective-permute-start.11 = (s16[784,128]{1,0:T(8,128)(2,1)S(1)}, s16[784,128]{1,0:T(8,128)(2,1)S(1)}, u32[]{:S(2)}, u32[]{:S(2)}) collective-permute-start(s16[784,128]{1,0:T(8,128)(2,1)S(1)} %shard_map.47), channel_id=1, source_target_pairs={{0,2},{1,3},{2,0},{3,1},{4,6},{5,7},{6,4},{7,5},{8,10},{9,11},{10,... | collective-permute-start | bytes 602120 | tf_op jit(solution)/shard_map/ppermute | solution.py:180
where the time goes:
time: 105 us; the launch traced here: 103 us
  starting transfers between devices  54 us (51%)
  waiting for transfers between devices  17.5 us (17%)
  Pallas kernels  15.4 us (15%)
  blocking collectives  8.14 us (8%)
  local copies, waits for them, and re-layouts  7.61 us (7%)
    ppermute x14, starting transfers between devices, step(): return lax.ppermute(value, AXES, pairs)  54 us
    ppermute x14, waiting for transfers between devices, step(): return lax.ppermute(value, AXES, pairs)  17.5 us
    pallas_call x4, Pallas kernels, region(): pl.pallas_call(functools.partial(region_kernel, shift), out_shape=jax.Sha...  12 us
    all_gather x3, blocking collectives, both_cores(): lax.all_gather(value, 'col', axis=0, tiled=False, axis_index_groups=CORE_...  8.14 us
    unnamed x14, local copies, waits for them, and re-layouts  4.71 us
  transfers between devices with their start and end apart: 14, of which 4 were waited for; matrix products, arithmetic and copies ran while one was open for 2% of the time, Pallas kernels for 11%

commit v1 on v0

v1 whole, which is shorter than its diff:
```python
import functools

import jax
import jax.numpy as jnp
from jax import lax
from jax.experimental import pallas as pl
from jax.experimental.pallas import tpu as pltpu
from jax.sharding import PartitionSpec as P


BLK = 128
AXES = ("row", "col", "layer")
ROWS, XS, LAYERS = 8, 4, 4
KEPT = 6
EXTRA = 16
LEVELS = 32000.0


def table(move):
    pairs = []
    for r in range(ROWS):
        for x in range(XS):
            for z in range(2):
                for k in range(2):
                    for l in range(LAYERS):
                        r2, x2, z2, k2, l2 = move(r, x, z, k, l)
                        here = (r * 16 + x * 4 + z * 2 + k) * LAYERS + l
                        there = ((r2 % ROWS) * 16 + (x2 % XS) * 4 + z2 * 2 + k2) * LAYERS + l2
                        pairs.append((here, there))
    return pairs


ALONG_X = table(lambda r, x, z, k, l: (r, x + 1 - 2 * k, z, k, l))
ACROSS_Z = table(lambda r, x, z, k, l: (r, x, 1 - z, k, l ^ 2))
OTHER_CORE = table(lambda r, x, z, k, l: (r, x, z, 1 - k, l))
CORE_PAIRS = [[2 * i, 2 * i + 1] for i in range(8)]


def both_cores(value):
    return lax.all_gather(value, "col", axis=0, tiled=False, axis_index_groups=CORE_PAIRS)


def place(xs_ref, slab, row, rows, mask_ref, row_at, at):
    for g in range(2):
        column = pl.ds(pl.multiple_of(at * 2 * BLK + g * BLK, BLK), BLK)
        for i in range(rows):
            lines = pl.ds(pl.multiple_of((row_at + i) * BLK, BLK), BLK)
            part = slab[g, lines, :]
            stored = jnp.where(mask_ref[row_at + i, row * 2 + g] == 1, part, jnp.zeros_like(part))
            xs_ref[i * BLK:(i + 1) * BLK, column] = stored


def early_kernel(at_ref, mask_ref, *refs):
    slabs, refs = refs[:7], refs[7:]
    pieces, (out_ref, last_ref, xs_ref) = refs[:9], refs[9:]
    y, x, z, k = (at_ref[i] for i in range(4))
    d = 1 - 2 * k
    places = ((x, 0), (x - d, 0), (x + d, 0), (x, 1), (x - d, 1), (x + d, 1), (x + 2, 1))
    for slab, (x_at, zsel) in zip(slabs, places):
        row = 2 * lax.rem(x_at + 8, XS) + lax.rem(z + zsel, 2)
        place(xs_ref, slab, row, 8, mask_ref, 0, lax.rem(row - y + 8, ROWS))
    late = lax.rem(2 * lax.rem(x + 2, XS) + z - y + 8, ROWS)
    column = pl.ds(pl.multiple_of(late * 2 * BLK, BLK), 2 * BLK)
    xs_ref[:, column] = jnp.zeros((1024, 2 * BLK), jnp.bfloat16)
    whole = [pieces[i][...] for i in range(4)]
    whole.append(jnp.concatenate([pieces[4][...], pieces[5][...]], axis=0))
    whole += [pieces[i][...] for i in range(6, 9)]
    for i, piece in enumerate(whole):

        @pl.when(late == i)
        def _():
            last_ref[...] = piece

    def rows(i, carry):
        lines = pl.ds(pl.multiple_of(i * 2 * BLK, 2 * BLK), 2 * BLK)
        right = jnp.concatenate(whole, axis=0)
        out_ref[lines, :] = jnp.dot(xs_ref[lines, :], right, preferred_element_type=jnp.float32)
        return carry

    lax.fori_loop(0, 4, rows, 0)


SMEM = pl.BlockSpec(memory_space=pltpu.SMEM)
VMEM = pl.BlockSpec(memory_space=pltpu.VMEM)


def early(at, mask, slabs, pieces):
    return pl.pallas_call(
        early_kernel,
        out_shape=(
            jax.ShapeDtypeStruct((1024, 512), jnp.float32),
            jax.ShapeDtypeStruct((2 * BLK, 512), jnp.bfloat16),
        ),
        in_specs=[SMEM] * 2 + [VMEM] * 16,
        out_specs=(VMEM, VMEM),
        scratch_shapes=[pltpu.VMEM((1024, 2048), jnp.bfloat16)],
        compiler_params=pltpu.CompilerParams(vmem_limit_bytes=20 * 2**20),
        cost_estimate=pl.CostEstimate(flops=2 * 1024 * 2048 * 512, bytes_accessed=4 * 2**20, transcendentals=0),
        name="early",
    )(at, mask, *slabs, *pieces)


def kept(keep_ref, j):
    flags = [keep_ref[j * 2 + a, b] == 1 for a in range(2) for b in range(4)]
    spots, at = [], jnp.int32(0)
    for flag in flags:
        spots.append(pl.ds(pl.multiple_of(jnp.minimum(at, KEPT - 1) * BLK, BLK), BLK))
        at = at + flag.astype(jnp.int32)
    return flags, spots


def late_kernel(shifts, at_ref, mask_ref, keep_ref, slab_ref, last_ref, sum_ref, *refs):
    outs, xs_ref = refs[:-1], refs[-1]
    x, z, _, l = (at_ref[i] for i in range(1, 5))
    row = 2 * lax.rem(x + 2, XS) + z
    for shift, out_ref in zip(shifts, outs):
        j = lax.rem(l + shift, LAYERS)
        place(xs_ref, slab_ref, row, 2, mask_ref, j * 2, 0)
        lines = pl.ds(pl.multiple_of(j * 2 * BLK, 2 * BLK), 2 * BLK)
        value = sum_ref[lines, :] + jnp.dot(xs_ref[...], last_ref[...], preferred_element_type=jnp.float32)
        flags, spots = kept(keep_ref, j)
        blocks = [value[a * BLK:(a + 1) * BLK, b * BLK:(b + 1) * BLK] for a in range(2) for b in range(4)]
        if shift:
            top = jnp.zeros((8, BLK), jnp.float32)
            for flag, block in zip(flags, blocks):
                high = jnp.max(jnp.abs(block).reshape(BLK // 8, 8, BLK), axis=0)
                top = jnp.maximum(top, jnp.where(flag, high, 0.0))
            top = jnp.max(top, axis=(0, 1), keepdims=True)
            level = jnp.ceil(8.0 * jnp.log2(jnp.maximum(top, 1e-30)))
            level = jnp.broadcast_to(level, (EXTRA, BLK))
            factor = (jnp.exp2(level * -0.125) * LEVELS)[0:1, :]
            out_ref[pl.ds(KEPT * BLK, EXTRA), :] = level.astype(jnp.int32).astype(jnp.int16)
            blocks = [jnp.round(block * factor).astype(jnp.int32).astype(jnp.int16) for block in blocks]
        for flag, spot, block in zip(flags, spots, blocks):

            @pl.when(flag)
            def _():
                out_ref[spot, :] = block


def late(shifts, at, mask, keep, slab, last, total):
    coded = jax.ShapeDtypeStruct((KEPT * BLK + EXTRA, BLK), jnp.int16)
    plain = jax.ShapeDtypeStruct((KEPT * BLK, BLK), jnp.float32)
    return pl.pallas_call(
        functools.partial(late_kernel, shifts),
        out_shape=tuple(coded if shift else plain for shift in shifts),
        in_specs=[SMEM] * 3 + [VMEM] * 3,
        out_specs=tuple(VMEM for _ in shifts),
        scratch_shapes=[pltpu.VMEM((2 * BLK, 2 * BLK), jnp.bfloat16)],
        compiler_params=pltpu.CompilerParams(vmem_limit_bytes=12 * 2**20),
        cost_estimate=pl.CostEstimate(
            flops=len(shifts) * 2 * 256 * 256 * 512, bytes_accessed=len(shifts) * 2**20, transcendentals=0
        ),
    )(at, mask, keep, slab, last, total)


def finish_kernel(at_ref, keep_ref, own_ref, *refs):
    *got_refs, out_ref = refs
    l = at_ref[4]
    scales = []
    for got in got_refs:
        level = got[pl.ds(KEPT * BLK, EXTRA), :].astype(jnp.int32).astype(jnp.float32)
        scales.append((jnp.exp2(level * 0.125) * (1.0 / LEVELS))[0:1, :])
    at = jnp.int32(0)
    for a in range(2):
        for b in range(4):
            flag = keep_ref[l * 2 + a, b] == 1
            spot = pl.ds(pl.multiple_of(jnp.minimum(at, KEPT - 1) * BLK, BLK), BLK)
            total = own_ref[spot, :]
            for got, scale in zip(got_refs, scales):
                total = total + got[spot, :].astype(jnp.int32).astype(jnp.float32) * scale
            total = jnp.where(flag, total, 0.0)
            out_ref[a * BLK:(a + 1) * BLK, b * BLK:(b + 1) * BLK] = total.astype(jnp.bfloat16)
            at = at + flag.astype(jnp.int32)


def finish(at, keep, own, got):
    smem = pl.BlockSpec(memory_space=pltpu.SMEM)
    vmem = pl.BlockSpec(memory_space=pltpu.VMEM)
    return pl.pallas_call(
        finish_kernel,
        out_shape=jax.ShapeDtypeStruct((2 * BLK, 4 * BLK), jnp.bfloat16),
        in_specs=[smem, smem] + [vmem] * 4,
        out_specs=vmem,
        compiler_params=pltpu.CompilerParams(vmem_limit_bytes=8 * 2**20),
        cost_estimate=pl.CostEstimate(flops=2**20, bytes_accessed=2 * 2**20, transcendentals=0),
        name="finish",
    )(at, keep, own, *got)


def body(sign_iterate, square, pattern, keep):
    l = lax.axis_index("layer")
    y = lax.axis_index("row")
    c = lax.axis_index("col")
    k = c % 2
    at = jnp.stack([y, c // 4, (c // 2) % 2, k, l]).astype(jnp.int32)
    mask = lax.dynamic_slice(pattern, (y * 8, 0), (8, 64)).reshape(8, 16, 4)
    mask = lax.dynamic_index_in_dim(mask, l, 2, False)
    keep_here = lax.dynamic_slice(keep, (y * 8, c * 4), (8, 4))

    def step(value, pairs):
        return lax.ppermute(value, AXES, pairs)

    def down(value, shift):
        return step(value, table(lambda r, x, z, k, l: (r + shift, x, z, k, l)))

    z_send = lax.dynamic_slice_in_dim(sign_iterate, (l ^ 2) * BLK, BLK, 1)
    z_own = step(z_send, ACROSS_Z)
    s0 = lax.dynamic_index_in_dim(square.reshape(2, LAYERS, BLK, 512), l, 1, False).reshape(256, 512)
    s7 = down(s0, 1)
    s1 = down(s0, -1)
    s6 = down(s0, 2)
    s2 = down(s0, -2)
    z0 = both_cores(z_own)
    z1 = step(z0, ALONG_X)
    x0 = both_cores(lax.dynamic_slice_in_dim(sign_iterate, l * BLK, BLK, 1))
    x1 = step(x0, ALONG_X)
    s4a = down(s6[:BLK], 2)
    s4b = down(s2[BLK:], -2)
    z2 = step(z1, ALONG_X)
    s5 = down(s6, 1)
    s3 = down(s2, -1)
    x2 = step(x1, ALONG_X)
    x1o = step(x1, OTHER_CORE)
    z1o = step(z1, OTHER_CORE)
    total, last = early(at, mask, (x0, x1, x1o, z0, z1, z1o, z2), (s0, s1, s2, s3, s4a, s4b, s5, s6, s7))
    shifts = (2, 1, 3)
    parts = late(shifts, at, mask, keep_here, x2, last, total)
    got = []
    for shift, part in zip(shifts, parts):
        pairs = table(lambda r, x, z, k, l: (r, x, z, k, (l + shift) % LAYERS))
        got.append(step(part, pairs))
    (own,) = late((0,), at, mask, keep_here, x2, last, total)
    return finish(at, keep_here, own, got)


def solution(mesh):
    return jax.shard_map(
        body,
        mesh=mesh,
        in_specs=(P("row", "col"), P("row", "col"), P(), P()),
        out_specs=P(("row", "layer"), "col"),
        check_vma=False,
    )
```

time: 105 us -> 129 us (1.23)
  the two profiles are of different devices: /device:TPU:1 before, /device:TPU:18 now
where the time goes in v1:
time: 129 us
  starting transfers between devices  63.1 us (49%)
  waiting for transfers between devices  39.6 us (31%)
  Pallas kernels  10.9 us (8%)
  local copies, waits for them, and re-layouts  10.1 us (8%)
  blocking collectives  4.35 us (3%)
    ppermute x18, starting transfers between devices, step(): return lax.ppermute(value, AXES, pairs)  63.1 us
    ppermute x18, waiting for transfers between devices, step(): return lax.ppermute(value, AXES, pairs)  39.6 us
    pallas_call x1, Pallas kernels, early(): pl.pallas_call(early_kernel, out_shape=(jax.ShapeDtypeStruct((1024, 512),...  6.41 us
    unnamed x18, local copies, waits for them, and re-layouts  5.79 us
    all_gather x2, blocking collectives, both_cores(): lax.all_gather(value, 'col', axis=0, tiled=False, axis_index_groups=CORE_...  4.35 us
    pallas_call x2, Pallas kernels, late(): pl.pallas_call(functools.partial(late_kernel, shifts), out_shape=tuple((c...  2.98 us
  transfers between devices with their start and end apart: 18, of which 7 were waited for; matrix products, arithmetic and copies ran while one was open for 2% of the time, Pallas kernels for 6%

profile of v1, /device:TPU:18, one launch (start us, length us, event | category | flops | bytes accessed | tf_op | source)
XLA Modules:
  0.0 128.5 jit_solution(10956260124405147663)
XLA Ops:
  0.0 0.0 copy-start
  0.0 1.2 constant_dynamic-slice_fusion.1
  1.2 10.9 %collective-permute-start.3 = (bf16[1024,128]{1,0:T(8,128)(2,1)S(1)}, bf16[1024,128]{1,0:T(8,128)(2,1)S(1)}, u32[]{:S(2)}, u32[]{:S(2)}) collective-permute-start(bf16[1024,128]{1,0:T(8,128)(2,1)S(1)} %get-tuple-element.15), channel_id=1, source_target_pairs={{0,10},{1,11},{2,8},{3,9},{4,14},{5,15},{6,12},{7,13},{8,2},{9,3},... | collective-permute-start | bytes 786440 | tf_op jit(solution)/shard_map/ppermute | solution.py:202
  12.1 2.2 %all-gather = bf16[2048,128]{1,0:T(8,128)(2,1)S(1)} all-gather(bf16[1024,128]{1,0:T(8,128)(2,1)S(1)} %get-tuple-element.16), channel_id=2, replica_groups={{0,4},{8,12},{16,20},{24,28},{32,36},{40,44},{48,52},{56,60},{1,5},{9,1..., dimensions={0}, use_global_device_ids=true | all-gather | bytes 786432 | tf_op jit(solution)/shard_map/all_gather | solution.py:40
  14.3 3.4 %collective-permute-start = (bf16[2,1024,128]{2,1,0:T(8,128)(2,1)S(1)}, bf16[2,1024,128]{2,1,0:T(8,128)(2,1)}, u32[]{:S(2)}, u32[]{:S(2)}) collective-permute-start(bf16[2,1024,128]{2,1,0:T(8,128)(2,1)S(1)} %bitcast.14), channel_id=1, source_target_pairs={{0,16},{1,17},{2,18},{3,19},{4,52},{5,53},{6,54},{7,55},{8,24},{9,... | collective-permute-start | bytes 1572872 | tf_op jit(solution)/shard_map/ppermute | solution.py:202
  17.7 0.0 copy-done
  17.7 5.5 %collective-permute-done.3 = bf16[1024,128]{1,0:T(8,128)(2,1)S(1)} collective-permute-done((bf16[1024,128]{1,0:T(8,128)(2,1)S(1)}, bf16[1024,128]{1,0:T(8,128)(2,1)S(1)}, u32[]{:S(2)}, u32[]{:S(2)}) %collective-permute-start.3) | collective-permute-done | bytes 262176 | tf_op jit(solution)/shard_map/ppermute | solution.py:202
  23.3 2.2 %all-gather.1 = bf16[2048,128]{1,0:T(8,128)(2,1)S(1)} all-gather(bf16[1024,128]{1,0:T(8,128)(2,1)S(1)} %collective-permute-done.3), channel_id=3, replica_groups={{0,4},{8,12},{16,20},{24,28},{32,36},{40,44},{48,52},{56,60},{1,5},{9,1..., dimensions={0}, use_global_device_ids=true | all-gather | bytes 786432 | tf_op jit(solution)/shard_map/all_gather | solution.py:40
  25.4 3.4 %collective-permute-start.4 = (bf16[2,1024,128]{2,1,0:T(8,128)(2,1)S(1)}, bf16[2,1024,128]{2,1,0:T(8,128)(2,1)}, u32[]{:S(2)}, u32[]{:S(2)}) collective-permute-start(bf16[2,1024,128]{2,1,0:T(8,128)(2,1)S(1)} %bitcast.16), channel_id=1, source_target_pairs={{0,16},{1,17},{2,18},{3,19},{4,52},{5,53},{6,54},{7,55},{8,24},{9,... | collective-permute-start | bytes 1572872 | tf_op jit(solution)/shard_map/ppermute | solution.py:202
  28.8 5.7 %collective-permute-start.10 = (bf16[256,512]{1,0:T(8,128)(2,1)S(1)}, bf16[256,512]{1,0:T(8,128)(2,1)S(1)}, u32[]{:S(2)}, u32[]{:S(2)}) collective-permute-start(bf16[256,512]{1,0:T(8,128)(2,1)S(1)} %bitcast.18), channel_id=1, source_target_pairs={{0,128},{1,129},{2,130},{3,131},{4,132},{5,133},{6,134},{7,135},{8... | collective-permute-start | bytes 786440 | tf_op jit(solution)/shard_map/ppermute | solution.py:202
  34.6 1.9 %collective-permute-start.8 = (bf16[256,512]{1,0:T(8,128)(2,1)S(1)}, bf16[256,512]{1,0:T(8,128)(2,1)S(1)}, u32[]{:S(2)}, u32[]{:S(2)}) collective-permute-start(bf16[256,512]{1,0:T(8,128)(2,1)S(1)} %bitcast.19), channel_id=1, source_target_pairs={{0,384},{1,385},{2,386},{3,387},{4,388},{5,389},{6,390},{7,391},{8... | collective-permute-start | bytes 786440 | tf_op jit(solution)/shard_map/ppermute | solution.py:202
  36.5 2.6 %collective-permute-start.14 = (bf16[256,512]{1,0:T(8,128)(2,1)S(1)}, bf16[256,512]{1,0:T(8,128)(2,1)S(1)}, u32[]{:S(2)}, u32[]{:S(2)}) collective-permute-start(bf16[256,512]{1,0:T(8,128)(2,1)S(1)} %bitcast.20), channel_id=1, source_target_pairs={{0,64},{1,65},{2,66},{3,67},{4,68},{5,69},{6,70},{7,71},{8,72},{9,... | collective-permute-start | bytes 786440 | tf_op jit(solution)/shard_map/ppermute | solution.py:202
  39.1 6.8 %collective-permute-done.10.refs_14_ = bf16[256,512]{1,0:T(8,128)(2,1)S(1)} collective-permute-done((bf16[256,512]{1,0:T(8,128)(2,1)S(1)}, bf16[256,512]{1,0:T(8,128)(2,1)S(1)}, u32[]{:S(2)}, u32[]{:S(2)}) %collective-permute-start.10) | collective-permute-done | bytes 262176 | tf_op jit(solution)/shard_map/ppermute | solution.py:202
  45.9 2.8 %collective-permute-start.7 = (bf16[256,512]{1,0:T(8,128)(2,1)S(1)}, bf16[256,512]{1,0:T(8,128)(2,1)S(1)}, u32[]{:S(2)}, u32[]{:S(2)}) collective-permute-start(bf16[256,512]{1,0:T(8,128)(2,1)S(1)} %bitcast.21), channel_id=1, source_target_pairs={{0,448},{1,449},{2,450},{3,451},{4,452},{5,453},{6,454},{7,455},{8... | collective-permute-start | bytes 786440 | tf_op jit(solution)/shard_map/ppermute | solution.py:202
  48.7 1.7 %collective-permute-done.8.refs_9_ = bf16[256,512]{1,0:T(8,128)(2,1)S(1)} collective-permute-done((bf16[256,512]{1,0:T(8,128)(2,1)S(1)}, bf16[256,512]{1,0:T(8,128)(2,1)S(1)}, u32[]{:S(2)}, u32[]{:S(2)}) %collective-permute-start.8) | collective-permute-done | bytes 262176 | tf_op jit(solution)/shard_map/ppermute | solution.py:202
  50.3 4.0 %collective-permute-start.11 = (bf16[128,512]{1,0:T(8,128)(2,1)S(1)}, bf16[128,512]{1,0:T(8,128)(2,1)S(1)}, u32[]{:S(2)}, u32[]{:S(2)}) collective-permute-start(bf16[128,512]{1,0:T(8,128)(2,1)S(1)} %slice.8), channel_id=1, source_target_pairs={{0,128},{1,129},{2,130},{3,131},{4,132},{5,133},{6,134},{7,135},{8... | collective-permute-start | bytes 393224 | tf_op jit(solution)/shard_map/ppermute | solution.py:202
  54.3 0.0 collective-permute-done.14.refs_15_
  54.3 0.0 copy-start.1
  54.4 3.9 %collective-permute-start.13 = (bf16[256,512]{1,0:T(8,128)(2,1)S(1)}, bf16[256,512]{1,0:T(8,128)(2,1)S(1)}, u32[]{:S(2)}, u32[]{:S(2)}) collective-permute-start(bf16[256,512]{1,0:T(8,128)(2,1)S(1)} %collective-permute-done.10.refs_14_), channel_id=1, source_target_pairs={{0,64},{1,65},{2,66},{3,67},{4,68},{5,69},{6,70},{7,71},{8,72},{9,... | collective-permute-start | bytes 786440 | tf_op jit(solution)/shard_map/ppermute | solution.py:202
  58.3 0.0 collective-permute-done.refs_1_
  58.3 1.9 %collective-permute-start.2 = (bf16[2,1024,128]{2,1,0:T(8,128)(2,1)}, bf16[2,1024,128]{2,1,0:T(8,128)(2,1)}, u32[]{:S(2)}, u32[]{:S(2)}) collective-permute-start(bf16[2,1024,128]{2,1,0:T(8,128)(2,1)} %collective-permute-done.refs_1_), channel_id=1, source_target_pairs={{0,4},{1,5},{2,6},{3,7},{4,0},{5,1},{6,2},{7,3},{8,12},{9,13},{10,... | collective-permute-start | bytes 1572872 | tf_op jit(solution)/shard_map/ppermute | solution.py:202
  60.2 0.0 collective-permute-done.4.refs_4_
  60.2 2.4 %collective-permute-start.5 = (bf16[2,1024,128]{2,1,0:T(8,128)(2,1)}, bf16[2,1024,128]{2,1,0:T(8,128)(2,1)}, u32[]{:S(2)}, u32[]{:S(2)}) collective-permute-start(bf16[2,1024,128]{2,1,0:T(8,128)(2,1)} %collective-permute-done.4.refs_4_), channel_id=1, source_target_pairs={{0,4},{1,5},{2,6},{3,7},{4,0},{5,1},{6,2},{7,3},{8,12},{9,13},{10,... | collective-permute-start | bytes 1572872 | tf_op jit(solution)/shard_map/ppermute | solution.py:202
  62.6 0.0 collective-permute-done.7.refs_8_
  62.7 0.0 copy-start.3
  62.7 0.7 copy-done.3
  63.4 3.4 %collective-permute-start.6 = (bf16[2,1024,128]{2,1,0:T(8,128)(2,1)}, bf16[2,1024,128]{2,1,0:T(8,128)(2,1)}, u32[]{:S(2)}, u32[]{:S(2)}) collective-permute-start(bf16[2,1024,128]{2,1,0:T(8,128)(2,1)} %collective-permute-done.4.refs_4_), channel_id=1, source_target_pairs={{0,16},{1,17},{2,18},{3,19},{4,52},{5,53},{6,54},{7,55},{8,24},{9,... | collective-permute-start | bytes 1572872 | tf_op jit(solution)/shard_map/ppermute | solution.py:202
  66.8 0.0 collective-permute-done.11.refs_11_
  66.8 2.0 %collective-permute-start.12 = (bf16[128,512]{1,0:T(8,128)(2,1)S(1)}, bf16[128,512]{1,0:T(8,128)(2,1)S(1)}, u32[]{:S(2)}, u32[]{:S(2)}) collective-permute-start(bf16[128,512]{1,0:T(8,128)(2,1)S(1)} %slice.9), channel_id=1, source_target_pairs={{0,384},{1,385},{2,386},{3,387},{4,388},{5,389},{6,390},{7,391},{8... | collective-permute-start | bytes 393224 | tf_op jit(solution)/shard_map/ppermute | solution.py:202
  68.8 0.0 copy-done.1
  68.8 9.8 %collective-permute-done.12.refs_12_ = bf16[128,512]{1,0:T(8,128)(2,1)S(1)} collective-permute-done((bf16[128,512]{1,0:T(8,128)(2,1)S(1)}, bf16[128,512]{1,0:T(8,128)(2,1)S(1)}, u32[]{:S(2)}, u32[]{:S(2)}) %collective-permute-start.12) | collective-permute-done | bytes 131104 | tf_op jit(solution)/shard_map/ppermute | solution.py:202
  78.6 0.0 copy-start.7
  78.6 0.6 copy-done.7
  79.2 2.1 %collective-permute-start.1 = (bf16[2,1024,128]{2,1,0:T(8,128)(2,1)}, bf16[2,1024,128]{2,1,0:T(8,128)(2,1)S(1)}, u32[]{:S(2)}, u32[]{:S(2)}) collective-permute-start(bf16[2,1024,128]{2,1,0:T(8,128)(2,1)} %collective-permute-done.refs_1_), channel_id=1, source_target_pairs={{0,16},{1,17},{2,18},{3,19},{4,52},{5,53},{6,54},{7,55},{8,24},{9,... | collective-permute-start | bytes 1572872 | tf_op jit(solution)/shard_map/ppermute | solution.py:202
  81.3 0.0 collective-permute-done.13.refs_13_
  81.3 0.0 copy-start.5
  81.3 0.7 copy-done.5
  82.0 1.9 %collective-permute-start.9 = (bf16[256,512]{1,0:T(8,128)(2,1)S(1)}, bf16[256,512]{1,0:T(8,128)(2,1)}, u32[]{:S(2)}, u32[]{:S(2)}) collective-permute-start(bf16[256,512]{1,0:T(8,128)(2,1)S(1)} %collective-permute-done.8.refs_9_), channel_id=1, source_target_pairs={{0,448},{1,449},{2,450},{3,451},{4,452},{5,453},{6,454},{7,455},{8... | collective-permute-start | bytes 786440 | tf_op jit(solution)/shard_map/ppermute | solution.py:202
  84.0 0.7 constant_dynamic-slice_fusion.4
  84.7 0.7 copy.6
  85.4 0.8 constant_dynamic-slice_fusion.3
  86.1 0.1 copy.7
  86.2 0.8 dynamic_slice.20.keep_ref
  87.0 0.1 stack.23.at_ref
  87.0 6.1 %collective-permute-done.9.refs_10_ = bf16[256,512]{1,0:T(8,128)(2,1)} collective-permute-done((bf16[256,512]{1,0:T(8,128)(2,1)S(1)}, bf16[256,512]{1,0:T(8,128)(2,1)}, u32[]{:S(2)}, u32[]{:S(2)}) %collective-permute-start.9) | collective-permute-done | bytes 262176 | tf_op jit(solution)/shard_map/ppermute | solution.py:202
  93.2 0.0 collective-permute-done.2.refs_2_
  93.2 0.0 collective-permute-done.5.refs_5_
  93.2 0.0 collective-permute-done.6.refs_6_
  93.2 0.0 copy-start.2
  93.2 0.9 copy-done.2
  94.1 0.9 copy-done.4
  95.1 0.9 copy-done.6
  96.0 0.9 copy-done.8
  96.9 6.4 %early.1 = (f32[1024,512]{1,0:T(8,128)S(1)}, bf16[256,512]{1,0:T(8,128)(2,1)S(1)}) custom-call(s32[5]{0:T(128)S(1)} %stack.23.at_ref, s32[8,16]{1,0:T(8,128)S(1)} %bitcast.23, bf16[2,1024,128]{2,1,0:T(8,128)(2,1)S(1)} %bitcast.15, bf16[2,1024,128]{2,1,0:T(8,128)(2,1)} %collective-permute-done.refs_1_, bf16[2,1024,128]{2,1,0:T(8,128)(2,1)} %collective-permute-done.2.refs_2_, ...), custom_call_target="tpu_custom_call" | custom-call | flops 2147483648 | bytes 4194304 | tf_op jit(solution)/shard_map/early/pallas_call | solution.py:88
  103.4 0.0 collective-permute-done.1.slab_ref
  103.4 2.0 %shard_map.47 = (s16[784,128]{1,0:T(8,128)(2,1)S(1)}, s16[784,128]{1,0:T(8,128)(2,1)S(1)}, s16[784,128]{1,0:T(8,128)(2,1)S(1)}) custom-call(s32[5]{0:T(128)S(1)} %stack.23.at_ref, s32[8,16]{1,0:T(8,128)S(1)} %bitcast.24, s32[8,4]{1,0:T(8,128)S(1)} %dynamic_slice.20.keep_ref, bf16[2,1024,128]{2,1,0:T(8,128)(2,1)S(1)} %collective-permute-done.1.slab_ref, ...), custom_call_target="tpu_custom_call" | custom-call | flops 201326592 | bytes 3145728 | tf_op jit(solution)/shard_map/pallas_call | solution.py:144
  105.4 3.2 %collective-permute-start.15 = (s16[784,128]{1,0:T(8,128)(2,1)S(1)}, s16[784,128]{1,0:T(8,128)(2,1)S(1)}, u32[]{:S(2)}, u32[]{:S(2)}) collective-permute-start(s16[784,128]{1,0:T(8,128)(2,1)S(1)} %get-tuple-element.12), channel_id=1, source_target_pairs={{0,2},{1,3},{2,0},{3,1},{4,6},{5,7},{6,4},{7,5},{8,10},{9,11},{10,... | collective-permute-start | bytes 602120 | tf_op jit(solution)/shard_map/ppermute | solution.py:202
  108.6 2.8 %collective-permute-start.16 = (s16[784,128]{1,0:T(8,128)(2,1)S(1)}, s16[784,128]{1,0:T(8,128)(2,1)S(1)}, u32[]{:S(2)}, u32[]{:S(2)}) collective-permute-start(s16[784,128]{1,0:T(8,128)(2,1)S(1)} %get-tuple-element.13), channel_id=1, source_target_pairs={{0,1},{1,2},{2,3},{3,0},{4,5},{5,6},{6,7},{7,4},{8,9},{9,10},{10,1... | collective-permute-start | bytes 602120 | tf_op jit(solution)/shard_map/ppermute | solution.py:202
  111.5 4.8 %collective-permute-start.17 = (s16[784,128]{1,0:T(8,128)(2,1)S(1)}, s16[784,128]{1,0:T(8,128)(2,1)S(1)}, u32[]{:S(2)}, u32[]{:S(2)}) collective-permute-start(s16[784,128]{1,0:T(8,128)(2,1)S(1)} %get-tuple-element.14), channel_id=1, source_target_pairs={{0,3},{1,0},{2,1},{3,2},{4,7},{5,4},{6,5},{7,6},{8,11},{9,8},{10,9... | collective-permute-start | bytes 602120 | tf_op jit(solution)/shard_map/ppermute | solution.py:202
  116.3 0.9 shard_map.46.own_ref
  117.2 7.5 %collective-permute-done.15.refs_0_ = s16[784,128]{1,0:T(8,128)(2,1)S(1)} collective-permute-done((s16[784,128]{1,0:T(8,128)(2,1)S(1)}, s16[784,128]{1,0:T(8,128)(2,1)S(1)}, u32[]{:S(2)}, u32[]{:S(2)}) %collective-permute-start.15) | collective-permute-done | bytes 200736 | tf_op jit(solution)/shard_map/ppermute | solution.py:202
  124.7 0.0 collective-permute-done.16.refs_1_
  124.7 2.2 %collective-permute-done.17.refs_2_ = s16[784,128]{1,0:T(8,128)(2,1)S(1)} collective-permute-done((s16[784,128]{1,0:T(8,128)(2,1)S(1)}, s16[784,128]{1,0:T(8,128)(2,1)S(1)}, u32[]{:S(2)}, u32[]{:S(2)}) %collective-permute-start.17) | collective-permute-done | bytes 200736 | tf_op jit(solution)/shard_map/ppermute | solution.py:202
  127.0 1.6 %finish.1 = bf16[256,512]{1,0:T(8,128)(2,1)} custom-call(s32[5]{0:T(128)S(1)} %stack.23.at_ref, s32[8,4]{1,0:T(8,128)S(1)} %dynamic_slice.20.keep_ref, f32[768,128]{1,0:T(8,128)S(1)} %shard_map.46.own_ref, s16[784,128]{1,0:T(8,128)(2,1)S(1)} %collective-permute-done.15.refs_0_, s16[784,128]{1,0:T(8,128)(2,1)S(1)} %collective-permute-done.16.refs_1_, ...), custom_call_target="tpu_custom_call" | custom-call | flops 1048576 | bytes 2097152 | tf_op jit(solution)/shard_map/finish/pallas_call | solution.py:180
  (6 shorter events, 0.1 us)
Async XLA Ops:
  0.0 17.7 %copy-start = (bf16[1024,512]{1,0:T(8,128)(2,1)S(1)}, bf16[1024,512]{1,0:T(8,128)(2,1)}, u32[]{:S(2)}) copy-start(bf16[1024,512]{1,0:T(8,128)(2,1)} %param.5) | copy-start | bytes 3145732
  1.2 22.1 %collective-permute-start.3 = (bf16[1024,128]{1,0:T(8,128)(2,1)S(1)}, bf16[1024,128]{1,0:T(8,128)(2,1)S(1)}, u32[]{:S(2)}, u32[]{:S(2)}) collective-permute-start(bf16[1024,128]{1,0:T(8,128)(2,1)S(1)} %get-tuple-element.15), channel_id=1, source_target_pairs={{0,10},{1,11},{2,8},{3,9},{4,14},{5,15},{6,12},{7,13},{8,2},{9,3},... | collective-permute-start | bytes 786440 | tf_op jit(solution)/shard_map/ppermute | solution.py:202
  14.3 44.0 %collective-permute-start = (bf16[2,1024,128]{2,1,0:T(8,128)(2,1)S(1)}, bf16[2,1024,128]{2,1,0:T(8,128)(2,1)}, u32[]{:S(2)}, u32[]{:S(2)}) collective-permute-start(bf16[2,1024,128]{2,1,0:T(8,128)(2,1)S(1)} %bitcast.14), channel_id=1, source_target_pairs={{0,16},{1,17},{2,18},{3,19},{4,52},{5,53},{6,54},{7,55},{8,24},{9,... | collective-permute-start | bytes 1572872 | tf_op jit(solution)/shard_map/ppermute | solution.py:202
  25.4 34.8 %collective-permute-start.4 = (bf16[2,1024,128]{2,1,0:T(8,128)(2,1)S(1)}, bf16[2,1024,128]{2,1,0:T(8,128)(2,1)}, u32[]{:S(2)}, u32[]{:S(2)}) collective-permute-start(bf16[2,1024,128]{2,1,0:T(8,128)(2,1)S(1)} %bitcast.16), channel_id=1, source_target_pairs={{0,16},{1,17},{2,18},{3,19},{4,52},{5,53},{6,54},{7,55},{8,24},{9,... | collective-permute-start | bytes 1572872 | tf_op jit(solution)/shard_map/ppermute | solution.py:202
  28.8 17.0 %collective-permute-start.10 = (bf16[256,512]{1,0:T(8,128)(2,1)S(1)}, bf16[256,512]{1,0:T(8,128)(2,1)S(1)}, u32[]{:S(2)}, u32[]{:S(2)}) collective-permute-start(bf16[256,512]{1,0:T(8,128)(2,1)S(1)} %bitcast.18), channel_id=1, source_target_pairs={{0,128},{1,129},{2,130},{3,131},{4,132},{5,133},{6,134},{7,135},{8... | collective-permute-start | bytes 786440 | tf_op jit(solution)/shard_map/ppermute | solution.py:202
  34.6 15.8 %collective-permute-start.8 = (bf16[256,512]{1,0:T(8,128)(2,1)S(1)}, bf16[256,512]{1,0:T(8,128)(2,1)S(1)}, u32[]{:S(2)}, u32[]{:S(2)}) collective-permute-start(bf16[256,512]{1,0:T(8,128)(2,1)S(1)} %bitcast.19), channel_id=1, source_target_pairs={{0,384},{1,385},{2,386},{3,387},{4,388},{5,389},{6,390},{7,391},{8... | collective-permute-start | bytes 786440 | tf_op jit(solution)/shard_map/ppermute | solution.py:202
  36.5 17.8 %collective-permute-start.14 = (bf16[256,512]{1,0:T(8,128)(2,1)S(1)}, bf16[256,512]{1,0:T(8,128)(2,1)S(1)}, u32[]{:S(2)}, u32[]{:S(2)}) collective-permute-start(bf16[256,512]{1,0:T(8,128)(2,1)S(1)} %bitcast.20), channel_id=1, source_target_pairs={{0,64},{1,65},{2,66},{3,67},{4,68},{5,69},{6,70},{7,71},{8,72},{9,... | collective-permute-start | bytes 786440 | tf_op jit(solution)/shard_map/ppermute | solution.py:202
  45.9 16.8 %collective-permute-start.7 = (bf16[256,512]{1,0:T(8,128)(2,1)S(1)}, bf16[256,512]{1,0:T(8,128)(2,1)S(1)}, u32[]{:S(2)}, u32[]{:S(2)}) collective-permute-start(bf16[256,512]{1,0:T(8,128)(2,1)S(1)} %bitcast.21), channel_id=1, source_target_pairs={{0,448},{1,449},{2,450},{3,451},{4,452},{5,453},{6,454},{7,455},{8... | collective-permute-start | bytes 786440 | tf_op jit(solution)/shard_map/ppermute | solution.py:202
  50.3 16.5 %collective-permute-start.11 = (bf16[128,512]{1,0:T(8,128)(2,1)S(1)}, bf16[128,512]{1,0:T(8,128)(2,1)S(1)}, u32[]{:S(2)}, u32[]{:S(2)}) collective-permute-start(bf16[128,512]{1,0:T(8,128)(2,1)S(1)} %slice.8), channel_id=1, source_target_pairs={{0,128},{1,129},{2,130},{3,131},{4,132},{5,133},{6,134},{7,135},{8... | collective-permute-start | bytes 393224 | tf_op jit(solution)/shard_map/ppermute | solution.py:202
  54.3 14.4 %copy-start.1 = (bf16[256,512]{1,0:T(8,128)(2,1)}, bf16[256,512]{1,0:T(8,128)(2,1)S(1)}, u32[]{:S(2)}) copy-start(bf16[256,512]{1,0:T(8,128)(2,1)S(1)} %collective-permute-done.14.refs_15_) | copy-start | bytes 786436
  54.4 27.0 %collective-permute-start.13 = (bf16[256,512]{1,0:T(8,128)(2,1)S(1)}, bf16[256,512]{1,0:T(8,128)(2,1)S(1)}, u32[]{:S(2)}, u32[]{:S(2)}) collective-permute-start(bf16[256,512]{1,0:T(8,128)(2,1)S(1)} %collective-permute-done.10.refs_14_), channel_id=1, source_target_pairs={{0,64},{1,65},{2,66},{3,67},{4,68},{5,69},{6,70},{7,71},{8,72},{9,... | collective-permute-start | bytes 786440 | tf_op jit(solution)/shard_map/ppermute | solution.py:202
  58.3 34.9 %collective-permute-start.2 = (bf16[2,1024,128]{2,1,0:T(8,128)(2,1)}, bf16[2,1024,128]{2,1,0:T(8,128)(2,1)}, u32[]{:S(2)}, u32[]{:S(2)}) collective-permute-start(bf16[2,1024,128]{2,1,0:T(8,128)(2,1)} %collective-permute-done.refs_1_), channel_id=1, source_target_pairs={{0,4},{1,5},{2,6},{3,7},{4,0},{5,1},{6,2},{7,3},{8,12},{9,13},{10,... | collective-permute-start | bytes 1572872 | tf_op jit(solution)/shard_map/ppermute | solution.py:202
  60.2 33.0 %collective-permute-start.5 = (bf16[2,1024,128]{2,1,0:T(8,128)(2,1)}, bf16[2,1024,128]{2,1,0:T(8,128)(2,1)}, u32[]{:S(2)}, u32[]{:S(2)}) collective-permute-start(bf16[2,1024,128]{2,1,0:T(8,128)(2,1)} %collective-permute-done.4.refs_4_), channel_id=1, source_target_pairs={{0,4},{1,5},{2,6},{3,7},{4,0},{5,1},{6,2},{7,3},{8,12},{9,13},{10,... | collective-permute-start | bytes 1572872 | tf_op jit(solution)/shard_map/ppermute | solution.py:202
  62.7 0.7 copy-start.3
  63.4 29.8 %collective-permute-start.6 = (bf16[2,1024,128]{2,1,0:T(8,128)(2,1)}, bf16[2,1024,128]{2,1,0:T(8,128)(2,1)}, u32[]{:S(2)}, u32[]{:S(2)}) collective-permute-start(bf16[2,1024,128]{2,1,0:T(8,128)(2,1)} %collective-permute-done.4.refs_4_), channel_id=1, source_target_pairs={{0,16},{1,17},{2,18},{3,19},{4,52},{5,53},{6,54},{7,55},{8,24},{9,... | collective-permute-start | bytes 1572872 | tf_op jit(solution)/shard_map/ppermute | solution.py:202
  66.8 11.8 %collective-permute-start.12 = (bf16[128,512]{1,0:T(8,128)(2,1)S(1)}, bf16[128,512]{1,0:T(8,128)(2,1)S(1)}, u32[]{:S(2)}, u32[]{:S(2)}) collective-permute-start(bf16[128,512]{1,0:T(8,128)(2,1)S(1)} %slice.9), channel_id=1, source_target_pairs={{0,384},{1,385},{2,386},{3,387},{4,388},{5,389},{6,390},{7,391},{8... | collective-permute-start | bytes 393224 | tf_op jit(solution)/shard_map/ppermute | solution.py:202
  78.6 0.6 copy-start.7
  79.2 24.2 %collective-permute-start.1 = (bf16[2,1024,128]{2,1,0:T(8,128)(2,1)}, bf16[2,1024,128]{2,1,0:T(8,128)(2,1)S(1)}, u32[]{:S(2)}, u32[]{:S(2)}) collective-permute-start(bf16[2,1024,128]{2,1,0:T(8,128)(2,1)} %collective-permute-done.refs_1_), channel_id=1, source_target_pairs={{0,16},{1,17},{2,18},{3,19},{4,52},{5,53},{6,54},{7,55},{8,24},{9,... | collective-permute-start | bytes 1572872 | tf_op jit(solution)/shard_map/ppermute | solution.py:202
  81.3 0.7 copy-start.5
  82.0 11.2 %collective-permute-start.9 = (bf16[256,512]{1,0:T(8,128)(2,1)S(1)}, bf16[256,512]{1,0:T(8,128)(2,1)}, u32[]{:S(2)}, u32[]{:S(2)}) collective-permute-start(bf16[256,512]{1,0:T(8,128)(2,1)S(1)} %collective-permute-done.8.refs_9_), channel_id=1, source_target_pairs={{0,448},{1,449},{2,450},{3,451},{4,452},{5,453},{6,454},{7,455},{8... | collective-permute-start | bytes 786440 | tf_op jit(solution)/shard_map/ppermute | solution.py:202
  93.2 1.0 copy-start.2
  94.1 0.9 copy-start.4
  95.1 0.9 copy-start.6
  96.0 0.9 copy-start.8
  105.4 19.3 %collective-permute-start.15 = (s16[784,128]{1,0:T(8,128)(2,1)S(1)}, s16[784,128]{1,0:T(8,128)(2,1)S(1)}, u32[]{:S(2)}, u32[]{:S(2)}) collective-permute-start(s16[784,128]{1,0:T(8,128)(2,1)S(1)} %get-tuple-element.12), channel_id=1, source_target_pairs={{0,2},{1,3},{2,0},{3,1},{4,6},{5,7},{6,4},{7,5},{8,10},{9,11},{10,... | collective-permute-start | bytes 602120 | tf_op jit(solution)/shard_map/ppermute | solution.py:202
  108.6 16.1 %collective-permute-start.16 = (s16[784,128]{1,0:T(8,128)(2,1)S(1)}, s16[784,128]{1,0:T(8,128)(2,1)S(1)}, u32[]{:S(2)}, u32[]{:S(2)}) collective-permute-start(s16[784,128]{1,0:T(8,128)(2,1)S(1)} %get-tuple-element.13), channel_id=1, source_target_pairs={{0,1},{1,2},{2,3},{3,0},{4,5},{5,6},{6,7},{7,4},{8,9},{9,10},{10,1... | collective-permute-start | bytes 602120 | tf_op jit(solution)/shard_map/ppermute | solution.py:202
  111.5 15.5 %collective-permute-start.17 = (s16[784,128]{1,0:T(8,128)(2,1)S(1)}, s16[784,128]{1,0:T(8,128)(2,1)S(1)}, u32[]{:S(2)}, u32[]{:S(2)}) collective-permute-start(s16[784,128]{1,0:T(8,128)(2,1)S(1)} %get-tuple-element.14), channel_id=1, source_target_pairs={{0,3},{1,0},{2,1},{3,2},{4,7},{5,4},{6,5},{7,6},{8,11},{9,8},{10,9... | collective-permute-start | bytes 602120 | tf_op jit(solution)/shard_map/ppermute | solution.py:202

commit v2 on v1

v2 whole, which is shorter than its diff:
```python
import functools

import jax
import jax.numpy as jnp
from jax import lax
from jax.experimental import pallas as pl
from jax.experimental.pallas import tpu as pltpu
from jax.sharding import PartitionSpec as P


BLK = 128
AXES = ("row", "col", "layer")
ROWS, XS, LAYERS = 8, 4, 4
KEPT = 6
EXTRA = 16
LEVELS = 32000.0


def table(move):
    pairs = []
    for r in range(ROWS):
        for x in range(XS):
            for z in range(2):
                for k in range(2):
                    for l in range(LAYERS):
                        r2, x2, z2, k2, l2 = move(r, x, z, k, l)
                        here = (r * 16 + x * 4 + z * 2 + k) * LAYERS + l
                        there = ((r2 % ROWS) * 16 + (x2 % XS) * 4 + z2 * 2 + k2) * LAYERS + l2
                        pairs.append((here, there))
    return pairs


ALONG_X = table(lambda r, x, z, k, l: (r, x + 1 - 2 * k, z, k, l))
ACROSS_Z = table(lambda r, x, z, k, l: (r, x, 1 - z, k, l ^ 2))
OTHER_CORE = table(lambda r, x, z, k, l: (r, x, z, 1 - k, l))
CORE_PAIRS = [[2 * i, 2 * i + 1] for i in range(8)]


def both_cores(value):
    return lax.all_gather(value, "col", axis=0, tiled=False, axis_index_groups=CORE_PAIRS)


def place(xs_ref, slab, row, at, pattern_ref, y, l):
    for g in range(2):
        column = pl.ds(pl.multiple_of(at * 2 * BLK + g * BLK, BLK), BLK)
        for i in range(8):
            part = slab[g, i * BLK:(i + 1) * BLK, :]
            stored = pattern_ref[y * 8 + i, (row * 2 + g) * LAYERS + l] == 1
            xs_ref[i * BLK:(i + 1) * BLK, column] = jnp.where(stored, part, jnp.zeros_like(part))


def early_kernel(at_ref, pattern_ref, *refs):
    slabs, refs = refs[:8], refs[8:]
    (s0_ref, d1_ref, d2_ref, d3_ref, s4_ref), (out_ref, xs_ref) = refs[:5], refs[5:]
    y, x, z, k, l = (at_ref[i] for i in range(5))
    d = 1 - 2 * k
    places = [(x_at, zsel) for zsel in range(2) for x_at in (x, x - d, x + d, x + 2)]
    for slab, (x_at, zsel) in zip(slabs, places):
        row = 2 * lax.rem(x_at + 8, XS) + lax.rem(z + zsel, 2)
        step = lax.rem(d * (y - row) + 16, ROWS)
        at = jnp.where(step <= 4, step, 12 - step)
        place(xs_ref, slab, row, at, pattern_ref, y, l)

    def rows(i, carry):
        lines = pl.ds(pl.multiple_of(i * 2 * BLK, 2 * BLK), 2 * BLK)
        right = jnp.concatenate([s0_ref[...], d1_ref[k], d2_ref[k], d3_ref[k], s4_ref[...]], axis=0)
        out_ref[lines, :] = jnp.dot(xs_ref[lines, :5 * 2 * BLK], right, preferred_element_type=jnp.float32)
        return carry

    lax.fori_loop(0, 4, rows, 0)


SMEM = pl.BlockSpec(memory_space=pltpu.SMEM)
VMEM = pl.BlockSpec(memory_space=pltpu.VMEM)


def early(at, pattern, slabs, pieces):
    return pl.pallas_call(
        early_kernel,
        out_shape=(
            jax.ShapeDtypeStruct((1024, 512), jnp.float32),
            jax.ShapeDtypeStruct((1024, 2048), jnp.bfloat16),
        ),
        in_specs=[SMEM] * 2 + [VMEM] * 13,
        out_specs=(VMEM, VMEM),
        compiler_params=pltpu.CompilerParams(vmem_limit_bytes=13 * 2**20),
        cost_estimate=pl.CostEstimate(flops=2 * 1024 * 1280 * 512, bytes_accessed=4 * 2**20, transcendentals=0),
        name="early",
    )(at, pattern, *slabs, *pieces)


def kept(keep_ref, at_ref, j):
    y, c = at_ref[0], at_ref[5]
    flags = [keep_ref[y * 8 + j * 2 + a, c * 4 + b] == 1 for a in range(2) for b in range(4)]
    spots, at = [], jnp.int32(0)
    for flag in flags:
        spots.append(pl.ds(pl.multiple_of(jnp.minimum(at, KEPT - 1) * BLK, BLK), BLK))
        at = at + flag.astype(jnp.int32)
    return flags, spots


def late_kernel(shifts, at_ref, keep_ref, swapped_ref, sum_ref, xs_ref, *outs):
    l = at_ref[4]
    for shift, out_ref in zip(shifts, outs):
        j = lax.rem(l + shift, LAYERS)
        lines = pl.ds(pl.multiple_of(j * 2 * BLK, 2 * BLK), 2 * BLK)
        right = swapped_ref[...].reshape(6 * BLK, 512)
        value = sum_ref[lines, :] + jnp.dot(xs_ref[lines, 10 * BLK:], right, preferred_element_type=jnp.float32)
        flags, spots = kept(keep_ref, at_ref, j)
        blocks = [value[a * BLK:(a + 1) * BLK, b * BLK:(b + 1) * BLK] for a in range(2) for b in range(4)]
        if shift:
            top = jnp.zeros((8, BLK), jnp.float32)
            for flag, block in zip(flags, blocks):
                high = jnp.max(jnp.abs(block).reshape(BLK // 8, 8, BLK), axis=0)
                top = jnp.maximum(top, jnp.where(flag, high, 0.0))
            top = jnp.max(top, axis=(0, 1), keepdims=True)
            level = jnp.ceil(8.0 * jnp.log2(jnp.maximum(top, 1e-30)))
            level = jnp.broadcast_to(level, (EXTRA, BLK))
            factor = (jnp.exp2(level * -0.125) * LEVELS)[0:1, :]
            out_ref[pl.ds(KEPT * BLK, EXTRA), :] = level.astype(jnp.int32).astype(jnp.int16)
            blocks = [jnp.round(block * factor).astype(jnp.int32).astype(jnp.int16) for block in blocks]
        for flag, spot, block in zip(flags, spots, blocks):

            @pl.when(flag)
            def _():
                out_ref[spot, :] = block


def late(shifts, at, keep, swapped, total, xs):
    coded = jax.ShapeDtypeStruct((KEPT * BLK + EXTRA, BLK), jnp.int16)
    plain = jax.ShapeDtypeStruct((KEPT * BLK, BLK), jnp.float32)
    return pl.pallas_call(
        functools.partial(late_kernel, shifts),
        out_shape=tuple(coded if shift else plain for shift in shifts),
        in_specs=[SMEM] * 2 + [VMEM] * 3,
        out_specs=tuple(VMEM for _ in shifts),
        compiler_params=pltpu.CompilerParams(vmem_limit_bytes=12 * 2**20),
        cost_estimate=pl.CostEstimate(
            flops=len(shifts) * 2 * 256 * 768 * 512, bytes_accessed=len(shifts) * 2**20, transcendentals=0
        ),
    )(at, keep, swapped, total, xs)


def finish_kernel(at_ref, keep_ref, own_ref, *refs):
    *got_refs, out_ref = refs
    l = at_ref[4]
    scales = []
    for got in got_refs:
        level = got[pl.ds(KEPT * BLK, EXTRA), :].astype(jnp.int32).astype(jnp.float32)
        scales.append((jnp.exp2(level * 0.125) * (1.0 / LEVELS))[0:1, :])
    flags, spots = kept(keep_ref, at_ref, l)
    for a in range(2):
        for b in range(4):
            flag, spot = flags[a * 4 + b], spots[a * 4 + b]
            total = own_ref[spot, :]
            for got, scale in zip(got_refs, scales):
                total = total + got[spot, :].astype(jnp.int32).astype(jnp.float32) * scale
            total = jnp.where(flag, total, 0.0)
            out_ref[a * BLK:(a + 1) * BLK, b * BLK:(b + 1) * BLK] = total.astype(jnp.bfloat16)


def finish(at, keep, own, got):
    smem = pl.BlockSpec(memory_space=pltpu.SMEM)
    vmem = pl.BlockSpec(memory_space=pltpu.VMEM)
    return pl.pallas_call(
        finish_kernel,
        out_shape=jax.ShapeDtypeStruct((2 * BLK, 4 * BLK), jnp.bfloat16),
        in_specs=[smem, smem] + [vmem] * 4,
        out_specs=vmem,
        compiler_params=pltpu.CompilerParams(vmem_limit_bytes=8 * 2**20),
        cost_estimate=pl.CostEstimate(flops=2**20, bytes_accessed=2 * 2**20, transcendentals=0),
        name="finish",
    )(at, keep, own, *got)


def body(sign_iterate, square, pattern, keep):
    l = lax.axis_index("layer")
    y = lax.axis_index("row")
    c = lax.axis_index("col")
    k = c % 2
    at = jnp.stack([y, c // 4, (c // 2) % 2, k, l, c]).astype(jnp.int32)

    def step(value, pairs):
        return lax.ppermute(value, AXES, pairs)

    def along(value, far):
        return step(value, table(lambda r, x, z, k, l: (r + far * (1 - 2 * k), x, z, k, l)))

    z_send = lax.dynamic_slice_in_dim(sign_iterate, (l ^ 2) * BLK, BLK, 1)
    z_own = step(z_send, ACROSS_Z)
    s0 = lax.dynamic_index_in_dim(square.reshape(2, LAYERS, BLK, 512), l, 1, False).reshape(256, 512)
    s_both = both_cores(s0)
    d1 = along(s_both, 1)
    x0 = both_cores(lax.dynamic_slice_in_dim(sign_iterate, l * BLK, BLK, 1))
    x1 = step(x0, ALONG_X)
    z0 = both_cores(z_own)
    z1 = step(z0, ALONG_X)
    d2 = along(s_both, 2)
    d3 = along(d1, 2)
    x2 = step(x1, ALONG_X)
    s4 = along(s0, 4)
    z2 = step(z1, ALONG_X)
    x1o = step(x1, OTHER_CORE)
    z1o = step(z1, OTHER_CORE)
    swapped = jnp.stack([lax.dynamic_index_in_dim(v, 1 - k, 0, False) for v in (d1, d2, d3)])
    swapped = step(swapped, OTHER_CORE)
    total, xs = early(at, pattern, (x0, x1, x1o, x2, z0, z1, z1o, z2), (s0, d1, d2, d3, s4))
    shifts = (2, 1, 3)
    parts = late(shifts, at, keep, swapped, total, xs)
    got = []
    for shift, part in zip(shifts, parts):
        pairs = table(lambda r, x, z, k, l: (r, x, z, k, (l + shift) % LAYERS))
        got.append(step(part, pairs))
    (own,) = late((0,), at, keep, swapped, total, xs)
    return finish(at, keep, own, got)


def solution(mesh):
    return jax.shard_map(
        body,
        mesh=mesh,
        in_specs=(P("row", "col"), P("row", "col"), P(), P()),
        out_specs=P(("row", "layer"), "col"),
        check_vma=False,
    )
```

time: 129 us -> 112 us (0.87)
  the two profiles are of different devices: /device:TPU:18 before, /device:TPU:15 now
where the time goes in v2:
time: 112 us; the launch traced here: 111 us
  starting transfers between devices  63.8 us (57%)
  waiting for transfers between devices  19.2 us (17%)
  Pallas kernels  12.4 us (11%)
  blocking collectives  9.27 us (8%)
  local copies, waits for them, and re-layouts  5.43 us (5%)
    ppermute x15, starting transfers between devices, step(): return lax.ppermute(value, AXES, pairs)  63.8 us
    ppermute x15, waiting for transfers between devices, step(): return lax.ppermute(value, AXES, pairs)  19.2 us
    all_gather x3, blocking collectives, both_cores(): lax.all_gather(value, 'col', axis=0, tiled=False, axis_index_groups=CORE_...  9.27 us
    pallas_call x1, Pallas kernels, early(): pl.pallas_call(early_kernel, out_shape=(jax.ShapeDtypeStruct((1024, 512),...  5.98 us
    pallas_call x2, Pallas kernels, late(): pl.pallas_call(functools.partial(late_kernel, shifts), out_shape=tuple((c...  4.38 us
    unnamed x10, local copies, waits for them, and re-layouts  2.28 us
  transfers between devices with their start and end apart: 15, of which 4 were waited for; matrix products, arithmetic and copies ran while one was open for 4% of the time, Pallas kernels for 7%

profile of v2, /device:TPU:15, one launch (start us, length us, event | category | flops | bytes accessed | tf_op | source)
XLA Modules:
  0.0 111.4 jit_solution(8790995956463219699)
XLA Ops:
  0.0 0.0 copy-start
  0.0 0.0 copy-start.4
  0.0 1.2 %copy-done = bf16[1024,512]{1,0:T(8,128)(2,1)S(1)} copy-done((bf16[1024,512]{1,0:T(8,128)(2,1)S(1)}, bf16[1024,512]{1,0:T(8,128)(2,1)}, u32[]{:S(2)}) %copy-start) | copy-done | bytes 1048600
  1.2 2.6 %all_gather.15 = bf16[2,256,512]{2,1,0:T(8,128)(2,1)} all-gather(bf16[1,256,512]{2,1,0:T(8,128)(2,1)S(1)} %bitcast.15), channel_id=1, replica_groups={{0,4},{8,12},{16,20},{24,28},{32,36},{40,44},{48,52},{56,60},{1,5},{9,1..., dimensions={0}, use_global_device_ids=true | all-gather | bytes 786432 | tf_op jit(solution)/shard_map/all_gather | solution.py:40
  3.9 2.1 %collective-permute-start = (bf16[2,256,512]{2,1,0:T(8,128)(2,1)}, bf16[2,256,512]{2,1,0:T(8,128)(2,1)S(1)}, u32[]{:S(2)}, u32[]{:S(2)}) collective-permute-start(bf16[2,256,512]{2,1,0:T(8,128)(2,1)} %all_gather.15), channel_id=1, source_target_pairs={{0,64},{1,65},{2,66},{3,67},{4,452},{5,453},{6,454},{7,455},{8,72}... | collective-permute-start | bytes 1572872 | tf_op jit(solution)/shard_map/ppermute | solution.py:184
  5.9 5.9 %collective-permute-start.1 = (bf16[2,256,512]{2,1,0:T(8,128)(2,1)}, bf16[2,256,512]{2,1,0:T(8,128)(2,1)}, u32[]{:S(2)}, u32[]{:S(2)}) collective-permute-start(bf16[2,256,512]{2,1,0:T(8,128)(2,1)} %all_gather.15), channel_id=1, source_target_pairs={{0,128},{1,129},{2,130},{3,131},{4,388},{5,389},{6,390},{7,391},{8... | collective-permute-start | bytes 1572872 | tf_op jit(solution)/shard_map/ppermute | solution.py:184
  11.8 1.1 constant_dynamic-slice_fusion
  12.9 10.7 %collective-permute-start.7 = (bf16[1024,128]{1,0:T(8,128)(2,1)S(1)}, bf16[1024,128]{1,0:T(8,128)(2,1)}, u32[]{:S(2)}, u32[]{:S(2)}) collective-permute-start(bf16[1024,128]{1,0:T(8,128)(2,1)S(1)} %get-tuple-element.15), channel_id=1, source_target_pairs={{0,10},{1,11},{2,8},{3,9},{4,14},{5,15},{6,12},{7,13},{8,2},{9,3},... | collective-permute-start | bytes 786440 | tf_op jit(solution)/shard_map/ppermute | solution.py:184
  23.6 0.0 collective-permute-done.refs_9_
  23.6 0.0 copy-start.1
  23.6 3.8 %collective-permute-start.2 = (bf16[2,256,512]{2,1,0:T(8,128)(2,1)S(1)}, bf16[2,256,512]{2,1,0:T(8,128)(2,1)}, u32[]{:S(2)}, u32[]{:S(2)}) collective-permute-start(bf16[2,256,512]{2,1,0:T(8,128)(2,1)S(1)} %collective-permute-done.refs_9_), channel_id=1, source_target_pairs={{0,128},{1,129},{2,130},{3,131},{4,388},{5,389},{6,390},{7,391},{8... | collective-permute-start | bytes 1572872 | tf_op jit(solution)/shard_map/ppermute | solution.py:184
  27.4 2.6 %all-gather = bf16[2048,128]{1,0:T(8,128)(2,1)S(1)} all-gather(bf16[1024,128]{1,0:T(8,128)(2,1)S(1)} %get-tuple-element.16), channel_id=2, replica_groups={{0,4},{8,12},{16,20},{24,28},{32,36},{40,44},{48,52},{56,60},{1,5},{9,1..., dimensions={0}, use_global_device_ids=true | all-gather | bytes 786432 | tf_op jit(solution)/shard_map/all_gather | solution.py:40
  30.0 2.4 %collective-permute-start.4 = (bf16[2,1024,128]{2,1,0:T(8,128)(2,1)S(1)}, bf16[2,1024,128]{2,1,0:T(8,128)(2,1)}, u32[]{:S(2)}, u32[]{:S(2)}) collective-permute-start(bf16[2,1024,128]{2,1,0:T(8,128)(2,1)S(1)} %bitcast.18), channel_id=1, source_target_pairs={{0,16},{1,17},{2,18},{3,19},{4,52},{5,53},{6,54},{7,55},{8,24},{9,... | collective-permute-start | bytes 1572872 | tf_op jit(solution)/shard_map/ppermute | solution.py:184
  32.5 3.5 %collective-permute-start.11 = (bf16[256,512]{1,0:T(8,128)(2,1)S(1)}, bf16[256,512]{1,0:T(8,128)(2,1)S(1)}, u32[]{:S(2)}, u32[]{:S(2)}) collective-permute-start(bf16[256,512]{1,0:T(8,128)(2,1)S(1)} %bitcast.16), channel_id=1, source_target_pairs={{0,256},{1,257},{2,258},{3,259},{4,260},{5,261},{6,262},{7,263},{8... | collective-permute-start | bytes 786440 | tf_op jit(solution)/shard_map/ppermute | solution.py:184
  36.0 0.0 collective-permute-done.7
  36.0 4.0 %all-gather.1 = bf16[2048,128]{1,0:T(8,128)(2,1)S(1)} all-gather(bf16[1024,128]{1,0:T(8,128)(2,1)} %collective-permute-done.7), channel_id=3, replica_groups={{0,4},{8,12},{16,20},{24,28},{32,36},{40,44},{48,52},{56,60},{1,5},{9,1..., dimensions={0}, use_global_device_ids=true | all-gather | bytes 786432 | tf_op jit(solution)/shard_map/all_gather | solution.py:40
  40.1 1.9 %collective-permute-start.8 = (bf16[2,1024,128]{2,1,0:T(8,128)(2,1)S(1)}, bf16[2,1024,128]{2,1,0:T(8,128)(2,1)}, u32[]{:S(2)}, u32[]{:S(2)}) collective-permute-start(bf16[2,1024,128]{2,1,0:T(8,128)(2,1)S(1)} %bitcast.20), channel_id=1, source_target_pairs={{0,16},{1,17},{2,18},{3,19},{4,52},{5,53},{6,54},{7,55},{8,24},{9,... | collective-permute-start | bytes 1572872 | tf_op jit(solution)/shard_map/ppermute | solution.py:184
  42.0 0.0 collective-permute-done.1.refs_10_
  42.0 1.0 constant_dynamic-slice_fusion.3
  43.0 0.0 copy-start.3
  43.0 0.0 collective-permute-done.2.refs_11_
  43.0 1.0 constant_dynamic-slice_fusion.2
  44.0 0.0 copy-done.1
  44.0 1.0 pad_maximum_fusion
  45.0 14.4 %collective-permute-start.3 = (bf16[3,256,512]{2,1,0:T(8,128)(2,1)}, bf16[3,256,512]{2,1,0:T(8,128)(2,1)S(1)}, u32[]{:S(2)}, u32[]{:S(2)}) collective-permute-start(bf16[3,256,512]{2,1,0:T(8,128)(2,1)} %pad_maximum_fusion), channel_id=1, source_target_pairs={{0,4},{1,5},{2,6},{3,7},{4,0},{5,1},{6,2},{7,3},{8,12},{9,13},{10,... | collective-permute-start | bytes 2359304 | tf_op jit(solution)/shard_map/ppermute | solution.py:184
  59.4 0.0 collective-permute-done.4.refs_1_
  59.4 1.9 %collective-permute-start.5 = (bf16[2,1024,128]{2,1,0:T(8,128)(2,1)}, bf16[2,1024,128]{2,1,0:T(8,128)(2,1)}, u32[]{:S(2)}, u32[]{:S(2)}) collective-permute-start(bf16[2,1024,128]{2,1,0:T(8,128)(2,1)} %collective-permute-done.4.refs_1_), channel_id=1, source_target_pairs={{0,4},{1,5},{2,6},{3,7},{4,0},{5,1},{6,2},{7,3},{8,12},{9,13},{10,... | collective-permute-start | bytes 1572872 | tf_op jit(solution)/shard_map/ppermute | solution.py:184
  61.3 2.5 %collective-permute-start.6 = (bf16[2,1024,128]{2,1,0:T(8,128)(2,1)}, bf16[2,1024,128]{2,1,0:T(8,128)(2,1)}, u32[]{:S(2)}, u32[]{:S(2)}) collective-permute-start(bf16[2,1024,128]{2,1,0:T(8,128)(2,1)} %collective-permute-done.4.refs_1_), channel_id=1, source_target_pairs={{0,16},{1,17},{2,18},{3,19},{4,52},{5,53},{6,54},{7,55},{8,24},{9,... | collective-permute-start | bytes 1572872 | tf_op jit(solution)/shard_map/ppermute | solution.py:184
  63.8 0.0 collective-permute-done.8.refs_5_
  63.8 2.2 %collective-permute-start.10 = (bf16[2,1024,128]{2,1,0:T(8,128)(2,1)}, bf16[2,1024,128]{2,1,0:T(8,128)(2,1)}, u32[]{:S(2)}, u32[]{:S(2)}) collective-permute-start(bf16[2,1024,128]{2,1,0:T(8,128)(2,1)} %collective-permute-done.8.refs_5_), channel_id=1, source_target_pairs={{0,16},{1,17},{2,18},{3,19},{4,52},{5,53},{6,54},{7,55},{8,24},{9,... | collective-permute-start | bytes 1572872 | tf_op jit(solution)/shard_map/ppermute | solution.py:184
  66.0 0.0 collective-permute-done.11.refs_12_
  66.0 3.6 %collective-permute-start.9 = (bf16[2,1024,128]{2,1,0:T(8,128)(2,1)}, bf16[2,1024,128]{2,1,0:T(8,128)(2,1)}, u32[]{:S(2)}, u32[]{:S(2)}) collective-permute-start(bf16[2,1024,128]{2,1,0:T(8,128)(2,1)} %collective-permute-done.8.refs_5_), channel_id=1, source_target_pairs={{0,4},{1,5},{2,6},{3,7},{4,0},{5,1},{6,2},{7,3},{8,12},{9,13},{10,... | collective-permute-start | bytes 1572872 | tf_op jit(solution)/shard_map/ppermute | solution.py:184
  69.6 0.1 stack.33.at_ref
  69.7 0.0 collective-permute-done.5.refs_2_
  69.7 3.1 %collective-permute-done.6.refs_3_ = bf16[2,1024,128]{2,1,0:T(8,128)(2,1)} collective-permute-done((bf16[2,1024,128]{2,1,0:T(8,128)(2,1)}, bf16[2,1024,128]{2,1,0:T(8,128)(2,1)}, u32[]{:S(2)}, u32[]{:S(2)}) %collective-permute-start.6) | collective-permute-done | bytes 524320 | tf_op jit(solution)/shard_map/ppermute | solution.py:184
  72.8 5.6 %collective-permute-done.10.refs_7_ = bf16[2,1024,128]{2,1,0:T(8,128)(2,1)} collective-permute-done((bf16[2,1024,128]{2,1,0:T(8,128)(2,1)}, bf16[2,1024,128]{2,1,0:T(8,128)(2,1)}, u32[]{:S(2)}, u32[]{:S(2)}) %collective-permute-start.10) | collective-permute-done | bytes 524320 | tf_op jit(solution)/shard_map/ppermute | solution.py:184
  78.4 0.0 collective-permute-done.9.refs_6_
  78.4 0.0 copy-done.4
  78.4 0.0 copy-start.2
  78.4 1.0 copy-done.2
  79.5 6.0 %early.1 = (f32[1024,512]{1,0:T(8,128)S(1)}, bf16[1024,2048]{1,0:T(8,128)(2,1)S(1)}) custom-call(s32[6]{0:T(128)S(1)} %stack.33.at_ref, s32[64,64]{1,0:T(8,128)S(1)} %copy-done.4, bf16[2,1024,128]{2,1,0:T(8,128)(2,1)S(1)} %bitcast.19, bf16[2,1024,128]{2,1,0:T(8,128)(2,1)} %collective-permute-done.4.refs_1_, ...), custom_call_target="tpu_custom_call" | custom-call | flops 1342177280 | bytes 4194304 | tf_op jit(solution)/shard_map/early/pallas_call | solution.py:78
  85.4 0.0 collective-permute-done.3.swapped_ref
  85.5 0.0 copy-done.3
  85.5 2.9 %shard_map.47 = (s16[784,128]{1,0:T(8,128)(2,1)S(1)}, s16[784,128]{1,0:T(8,128)(2,1)S(1)}, s16[784,128]{1,0:T(8,128)(2,1)S(1)}) custom-call(s32[6]{0:T(128)S(1)} %stack.33.at_ref, s32[64,64]{1,0:T(8,128)S(1)} %copy-done.3, bf16[3,256,512]{2,1,0:T(8,128)(2,1)S(1)} %collective-permute-done.3.swapped_ref, f32[1024,512]{1,0:T(8,128)S(1)} %get-tuple-element.10.sum_ref, ...), custom_call_target="tpu_custom_call" | custom-call | flops 603979776 | bytes 3145728 | tf_op jit(solution)/shard_map/pallas_call | solution.py:132
  88.4 1.9 %collective-permute-start.12 = (s16[784,128]{1,0:T(8,128)(2,1)S(1)}, s16[784,128]{1,0:T(8,128)(2,1)S(1)}, u32[]{:S(2)}, u32[]{:S(2)}) collective-permute-start(s16[784,128]{1,0:T(8,128)(2,1)S(1)} %get-tuple-element.12), channel_id=1, source_target_pairs={{0,2},{1,3},{2,0},{3,1},{4,6},{5,7},{6,4},{7,5},{8,10},{9,11},{10,... | collective-permute-start | bytes 602120 | tf_op jit(solution)/shard_map/ppermute | solution.py:184
  90.3 1.9 %collective-permute-start.13 = (s16[784,128]{1,0:T(8,128)(2,1)S(1)}, s16[784,128]{1,0:T(8,128)(2,1)S(1)}, u32[]{:S(2)}, u32[]{:S(2)}) collective-permute-start(s16[784,128]{1,0:T(8,128)(2,1)S(1)} %get-tuple-element.13), channel_id=1, source_target_pairs={{0,1},{1,2},{2,3},{3,0},{4,5},{5,6},{6,7},{7,4},{8,9},{9,10},{10,1... | collective-permute-start | bytes 602120 | tf_op jit(solution)/shard_map/ppermute | solution.py:184
  92.2 5.2 %collective-permute-start.14 = (s16[784,128]{1,0:T(8,128)(2,1)S(1)}, s16[784,128]{1,0:T(8,128)(2,1)S(1)}, u32[]{:S(2)}, u32[]{:S(2)}) collective-permute-start(s16[784,128]{1,0:T(8,128)(2,1)S(1)} %get-tuple-element.14), channel_id=1, source_target_pairs={{0,3},{1,0},{2,1},{3,2},{4,7},{5,4},{6,5},{7,6},{8,11},{9,8},{10,9... | collective-permute-start | bytes 602120 | tf_op jit(solution)/shard_map/ppermute | solution.py:184
  97.4 1.5 %shard_map.46.own_ref = f32[768,128]{1,0:T(8,128)S(1)} custom-call(s32[6]{0:T(128)S(1)} %stack.33.at_ref, s32[64,64]{1,0:T(8,128)S(1)} %copy-done.3, bf16[3,256,512]{2,1,0:T(8,128)(2,1)S(1)} %collective-permute-done.3.swapped_ref, f32[1024,512]{1,0:T(8,128)S(1)} %get-tuple-element.10.sum_ref, bf16[1024,2048]{1,0:T(8,128)(2,1)S(1)} %get-tuple-element.11.xs_ref), custom_call_target="tpu_custom_call" | custom-call | flops 201326592 | bytes 1048576 | tf_op jit(solution)/shard_map/pallas_call | solution.py:132
  98.9 6.2 %collective-permute-done.12.refs_0_ = s16[784,128]{1,0:T(8,128)(2,1)S(1)} collective-permute-done((s16[784,128]{1,0:T(8,128)(2,1)S(1)}, s16[784,128]{1,0:T(8,128)(2,1)S(1)}, u32[]{:S(2)}, u32[]{:S(2)}) %collective-permute-start.12) | collective-permute-done | bytes 200736 | tf_op jit(solution)/shard_map/ppermute | solution.py:184
  105.1 0.0 collective-permute-done.13.refs_1_
  105.1 4.2 %collective-permute-done.14.refs_2_ = s16[784,128]{1,0:T(8,128)(2,1)S(1)} collective-permute-done((s16[784,128]{1,0:T(8,128)(2,1)S(1)}, s16[784,128]{1,0:T(8,128)(2,1)S(1)}, u32[]{:S(2)}, u32[]{:S(2)}) %collective-permute-start.14) | collective-permute-done | bytes 200736 | tf_op jit(solution)/shard_map/ppermute | solution.py:184
  109.4 2.0 %finish.1 = bf16[256,512]{1,0:T(8,128)(2,1)} custom-call(s32[6]{0:T(128)S(1)} %stack.33.at_ref, s32[64,64]{1,0:T(8,128)S(1)} %copy-done.3, f32[768,128]{1,0:T(8,128)S(1)} %shard_map.46.own_ref, s16[784,128]{1,0:T(8,128)(2,1)S(1)} %collective-permute-done.12.refs_0_, s16[784,128]{1,0:T(8,128)(2,1)S(1)} %collective-permute-done.13.refs_1_, ...), custom_call_target="tpu_custom_call" | custom-call | flops 1048576 | bytes 2097152 | tf_op jit(solution)/shard_map/finish/pallas_call | solution.py:165
  (2 shorter events, 0.0 us)
Async XLA Ops:
  0.0 1.2 %copy-start = (bf16[1024,512]{1,0:T(8,128)(2,1)S(1)}, bf16[1024,512]{1,0:T(8,128)(2,1)}, u32[]{:S(2)}) copy-start(bf16[1024,512]{1,0:T(8,128)(2,1)} %param.5) | copy-start | bytes 3145732
  0.0 78.4 %copy-start.4 = (s32[64,64]{1,0:T(8,128)S(1)}, s32[64,64]{1,0:T(8,128)}, u32[]{:S(2)}) copy-start(s32[64,64]{1,0:T(8,128)} %pattern_ref.1) | copy-start | bytes 49156
  3.9 19.7 %collective-permute-start = (bf16[2,256,512]{2,1,0:T(8,128)(2,1)}, bf16[2,256,512]{2,1,0:T(8,128)(2,1)S(1)}, u32[]{:S(2)}, u32[]{:S(2)}) collective-permute-start(bf16[2,256,512]{2,1,0:T(8,128)(2,1)} %all_gather.15), channel_id=1, source_target_pairs={{0,64},{1,65},{2,66},{3,67},{4,452},{5,453},{6,454},{7,455},{8,72}... | collective-permute-start | bytes 1572872 | tf_op jit(solution)/shard_map/ppermute | solution.py:184
  5.9 36.1 %collective-permute-start.1 = (bf16[2,256,512]{2,1,0:T(8,128)(2,1)}, bf16[2,256,512]{2,1,0:T(8,128)(2,1)}, u32[]{:S(2)}, u32[]{:S(2)}) collective-permute-start(bf16[2,256,512]{2,1,0:T(8,128)(2,1)} %all_gather.15), channel_id=1, source_target_pairs={{0,128},{1,129},{2,130},{3,131},{4,388},{5,389},{6,390},{7,391},{8... | collective-permute-start | bytes 1572872 | tf_op jit(solution)/shard_map/ppermute | solution.py:184
  12.9 23.1 %collective-permute-start.7 = (bf16[1024,128]{1,0:T(8,128)(2,1)S(1)}, bf16[1024,128]{1,0:T(8,128)(2,1)}, u32[]{:S(2)}, u32[]{:S(2)}) collective-permute-start(bf16[1024,128]{1,0:T(8,128)(2,1)S(1)} %get-tuple-element.15), channel_id=1, source_target_pairs={{0,10},{1,11},{2,8},{3,9},{4,14},{5,15},{6,12},{7,13},{8,2},{9,3},... | collective-permute-start | bytes 786440 | tf_op jit(solution)/shard_map/ppermute | solution.py:184
  23.6 20.4 %copy-start.1 = (bf16[2,256,512]{2,1,0:T(8,128)(2,1)}, bf16[2,256,512]{2,1,0:T(8,128)(2,1)S(1)}, u32[]{:S(2)}) copy-start(bf16[2,256,512]{2,1,0:T(8,128)(2,1)S(1)} %collective-permute-done.refs_9_) | copy-start | bytes 1572868
  23.6 19.4 %collective-permute-start.2 = (bf16[2,256,512]{2,1,0:T(8,128)(2,1)S(1)}, bf16[2,256,512]{2,1,0:T(8,128)(2,1)}, u32[]{:S(2)}, u32[]{:S(2)}) collective-permute-start(bf16[2,256,512]{2,1,0:T(8,128)(2,1)S(1)} %collective-permute-done.refs_9_), channel_id=1, source_target_pairs={{0,128},{1,129},{2,130},{3,131},{4,388},{5,389},{6,390},{7,391},{8... | collective-permute-start | bytes 1572872 | tf_op jit(solution)/shard_map/ppermute | solution.py:184
  30.0 29.4 %collective-permute-start.4 = (bf16[2,1024,128]{2,1,0:T(8,128)(2,1)S(1)}, bf16[2,1024,128]{2,1,0:T(8,128)(2,1)}, u32[]{:S(2)}, u32[]{:S(2)}) collective-permute-start(bf16[2,1024,128]{2,1,0:T(8,128)(2,1)S(1)} %bitcast.18), channel_id=1, source_target_pairs={{0,16},{1,17},{2,18},{3,19},{4,52},{5,53},{6,54},{7,55},{8,24},{9,... | collective-permute-start | bytes 1572872 | tf_op jit(solution)/shard_map/ppermute | solution.py:184
  32.5 33.5 %collective-permute-start.11 = (bf16[256,512]{1,0:T(8,128)(2,1)S(1)}, bf16[256,512]{1,0:T(8,128)(2,1)S(1)}, u32[]{:S(2)}, u32[]{:S(2)}) collective-permute-start(bf16[256,512]{1,0:T(8,128)(2,1)S(1)} %bitcast.16), channel_id=1, source_target_pairs={{0,256},{1,257},{2,258},{3,259},{4,260},{5,261},{6,262},{7,263},{8... | collective-permute-start | bytes 786440 | tf_op jit(solution)/shard_map/ppermute | solution.py:184
  40.1 23.8 %collective-permute-start.8 = (bf16[2,1024,128]{2,1,0:T(8,128)(2,1)S(1)}, bf16[2,1024,128]{2,1,0:T(8,128)(2,1)}, u32[]{:S(2)}, u32[]{:S(2)}) collective-permute-start(bf16[2,1024,128]{2,1,0:T(8,128)(2,1)S(1)} %bitcast.20), channel_id=1, source_target_pairs={{0,16},{1,17},{2,18},{3,19},{4,52},{5,53},{6,54},{7,55},{8,24},{9,... | collective-permute-start | bytes 1572872 | tf_op jit(solution)/shard_map/ppermute | solution.py:184
  43.0 42.5 %copy-start.3 = (s32[64,64]{1,0:T(8,128)S(1)}, s32[64,64]{1,0:T(8,128)}, u32[]{:S(2)}) copy-start(s32[64,64]{1,0:T(8,128)} %keep_ref.5) | copy-start | bytes 49156
  45.0 40.5 %collective-permute-start.3 = (bf16[3,256,512]{2,1,0:T(8,128)(2,1)}, bf16[3,256,512]{2,1,0:T(8,128)(2,1)S(1)}, u32[]{:S(2)}, u32[]{:S(2)}) collective-permute-start(bf16[3,256,512]{2,1,0:T(8,128)(2,1)} %pad_maximum_fusion), channel_id=1, source_target_pairs={{0,4},{1,5},{2,6},{3,7},{4,0},{5,1},{6,2},{7,3},{8,12},{9,13},{10,... | collective-permute-start | bytes 2359304 | tf_op jit(solution)/shard_map/ppermute | solution.py:184
  59.4 10.3 %collective-permute-start.5 = (bf16[2,1024,128]{2,1,0:T(8,128)(2,1)}, bf16[2,1024,128]{2,1,0:T(8,128)(2,1)}, u32[]{:S(2)}, u32[]{:S(2)}) collective-permute-start(bf16[2,1024,128]{2,1,0:T(8,128)(2,1)} %collective-permute-done.4.refs_1_), channel_id=1, source_target_pairs={{0,4},{1,5},{2,6},{3,7},{4,0},{5,1},{6,2},{7,3},{8,12},{9,13},{10,... | collective-permute-start | bytes 1572872 | tf_op jit(solution)/shard_map/ppermute | solution.py:184
  61.3 11.5 %collective-permute-start.6 = (bf16[2,1024,128]{2,1,0:T(8,128)(2,1)}, bf16[2,1024,128]{2,1,0:T(8,128)(2,1)}, u32[]{:S(2)}, u32[]{:S(2)}) collective-permute-start(bf16[2,1024,128]{2,1,0:T(8,128)(2,1)} %collective-permute-done.4.refs_1_), channel_id=1, source_target_pairs={{0,16},{1,17},{2,18},{3,19},{4,52},{5,53},{6,54},{7,55},{8,24},{9,... | collective-permute-start | bytes 1572872 | tf_op jit(solution)/shard_map/ppermute | solution.py:184
  63.8 14.6 %collective-permute-start.10 = (bf16[2,1024,128]{2,1,0:T(8,128)(2,1)}, bf16[2,1024,128]{2,1,0:T(8,128)(2,1)}, u32[]{:S(2)}, u32[]{:S(2)}) collective-permute-start(bf16[2,1024,128]{2,1,0:T(8,128)(2,1)} %collective-permute-done.8.refs_5_), channel_id=1, source_target_pairs={{0,16},{1,17},{2,18},{3,19},{4,52},{5,53},{6,54},{7,55},{8,24},{9,... | collective-permute-start | bytes 1572872 | tf_op jit(solution)/shard_map/ppermute | solution.py:184
  66.0 12.4 %collective-permute-start.9 = (bf16[2,1024,128]{2,1,0:T(8,128)(2,1)}, bf16[2,1024,128]{2,1,0:T(8,128)(2,1)}, u32[]{:S(2)}, u32[]{:S(2)}) collective-permute-start(bf16[2,1024,128]{2,1,0:T(8,128)(2,1)} %collective-permute-done.8.refs_5_), channel_id=1, source_target_pairs={{0,4},{1,5},{2,6},{3,7},{4,0},{5,1},{6,2},{7,3},{8,12},{9,13},{10,... | collective-permute-start | bytes 1572872 | tf_op jit(solution)/shard_map/ppermute | solution.py:184
  78.4 1.0 copy-start.2
  88.4 16.7 %collective-permute-start.12 = (s16[784,128]{1,0:T(8,128)(2,1)S(1)}, s16[784,128]{1,0:T(8,128)(2,1)S(1)}, u32[]{:S(2)}, u32[]{:S(2)}) collective-permute-start(s16[784,128]{1,0:T(8,128)(2,1)S(1)} %get-tuple-element.12), channel_id=1, source_target_pairs={{0,2},{1,3},{2,0},{3,1},{4,6},{5,7},{6,4},{7,5},{8,10},{9,11},{10,... | collective-permute-start | bytes 602120 | tf_op jit(solution)/shard_map/ppermute | solution.py:184
  90.3 14.8 %collective-permute-start.13 = (s16[784,128]{1,0:T(8,128)(2,1)S(1)}, s16[784,128]{1,0:T(8,128)(2,1)S(1)}, u32[]{:S(2)}, u32[]{:S(2)}) collective-permute-start(s16[784,128]{1,0:T(8,128)(2,1)S(1)} %get-tuple-element.13), channel_id=1, source_target_pairs={{0,1},{1,2},{2,3},{3,0},{4,5},{5,6},{6,7},{7,4},{8,9},{9,10},{10,1... | collective-permute-start | bytes 602120 | tf_op jit(solution)/shard_map/ppermute | solution.py:184
  92.2 17.1 %collective-permute-start.14 = (s16[784,128]{1,0:T(8,128)(2,1)S(1)}, s16[784,128]{1,0:T(8,128)(2,1)S(1)}, u32[]{:S(2)}, u32[]{:S(2)}) collective-permute-start(s16[784,128]{1,0:T(8,128)(2,1)S(1)} %get-tuple-element.14), channel_id=1, source_target_pairs={{0,3},{1,0},{2,1},{3,2},{4,7},{5,4},{6,5},{7,6},{8,11},{9,8},{10,9... | collective-permute-start | bytes 602120 | tf_op jit(solution)/shard_map/ppermute | solution.py:184
